TPU v7x, 256 devices: a whole 4x4x8 slice. The times are simulated.
256 devices in a mesh: gx: 32 (over z, x), gy: 4 (over y), blk: 2 (over core).
Axes of the slice: x: 4, y: 4, z: 8, core: 2. Of those that a mesh axis runs over, the one named last changes fastest.
Arguments:
- pressure: float32 [512, 256, 256], P('gx', 'gy', 'blk'), may hold values from -6 to 6
- pressure_prev: float32 [512, 256, 256], P('gx', 'gy', 'blk'), may hold values from -6 to 6
- buoyancy: float32 [512, 256, 256], P('gx', 'gy', 'blk'), may hold values from 0.5 to 2
- kappa: float32 [512, 256, 256], P('gx', 'gy', 'blk'), may hold values from 0.5 to 2
- hull_accel: float32 [131072, 128], P(('gx', 'gy', 'blk')), may hold values from -6 to 6
- row_block: int32 [131072, 1], P(('gx', 'gy', 'blk')), may hold values from 0 to 127; in each aligned block of 512 rows (0 to 511, 512 to 1023, ...) at most 8 rows name the same one
- row_column: int32 [131072, 1], P(('gx', 'gy', 'blk')), may hold values from 0 to 1023
Outputs:
- pressure_next: float32 [512, 256, 256], P('gx', 'gy', 'blk')
- hull_pressure: float32 [131072, 128], P(('gx', 'gy', 'blk'))
Inputs may be any that keep to these rules, and one draw needn't show every extreme that they name: `row_block`: among the 512 rows of one device at most 8 name the same block, and exactly 8 do for some block.
All inputs are finite; a program needn't handle non-finite values.
Results may differ from a plain program's by a relative error of at most 0.00002.
Values sent between devices are 32-bit elements; how exact they have to be, the bound alone decides.
A program may use at most 64 MiB of HBM per device.

v0:
```python
import functools

import jax
import jax.numpy as jnp
from jax import lax
from jax.experimental import pallas as pl
from jax.experimental.pallas import tpu as pltpu
from jax.sharding import PartitionSpec as P

MESH = pl.DeviceIdType.MESH
F32 = jnp.float32
BF16 = jnp.bfloat16
LANES = 128
CAP = 8
MSG = 9
COURANT = 0.05
GAIN = 0.5
FACE = COURANT * 0.5 / 576.0


def torus(n_gx, n_gy):
    nx = 4 if n_gx % 4 == 0 and n_gx > 4 else 2
    return n_gx // nx, nx, n_gy


def split2(v):
    hi = v.astype(BF16)
    lo = (v - hi.astype(F32)).astype(BF16)
    return hi, lo


def parts(v):
    hi, lo = split2(v)
    return jnp.concatenate([hi, lo], axis=1)


def joined(v):
    return v[:, :LANES] + v[:, LANES:]


def wide(a, b, c, d):
    return 27.0 * (c - b) - (d - a)


def dot(a, b):
    return jnp.dot(a, b, preferred_element_type=F32)


def dot_nt(a, b):
    return lax.dot_general(a, b, (((1,), (1,)), ((), ())), preferred_element_type=F32)


def dot_tn(a, b):
    return lax.dot_general(a, b, (((0,), (0,)), ((), ())), preferred_element_type=F32)


def onehot(mask):
    return jnp.where(mask, 1.0, 0.0).astype(BF16)


def kernel(
    dims,
    p_hbm, prev_hbm, b_hbm, kap_hbm, hull_hbm, rb_ref, rc_ref,
    out_hbm, hp_hbm,
    E, EB, E2, OP, OB, OM, PREV, KAP, HULL, FX, FY, BX, BY, BZ, BZO, SRC, NEXT,
    SB, RV, PK, RET, Q, PM, HOUT,
    in_sem, out_sem, hs_sem, hr_sem, ms_sem, mr_sem, as_sem, ar_sem, bs_sem, br_sem, self_sem,
):
    nz, nx, ny = dims
    NB = nz * nx * ny
    G = nx * ny
    GS = G * CAP
    X, Y = PREV.shape[0], PREV.shape[1]
    HR = HULL.shape[0]
    n_gx = nz * nx
    gx = lax.axis_index("gx")
    gy = lax.axis_index("gy")
    blk = lax.axis_index("blk")
    zi = gx // nx
    xi = gx % nx
    me = gx * ny + gy

    zs = [(zi + dz) % nz for dz in range(nz)]
    xs = [(xi + dx) % nx for dx in range(nx)]
    ys = [(gy + dy) % ny for dy in range(ny)]
    zb = [(zi + nz - dz) % nz for dz in range(nz)]
    xb = [(xi + nx - dx) % nx for dx in range(nx)]
    yb = [(gy + ny - dy) % ny for dy in range(ny)]
    half = nz // 2
    order = [half]
    for step in range(half - 1, 0, -1):
        order += [step, nz - step]
    order += [0]
    offsets = {dz: [(dx, dy) for dx in range(nx) for dy in range(ny)] for dz in range(nz)}

    barrier = pltpu.get_barrier_semaphore()
    for dz in order:
        for dx, dy in offsets[dz]:
            if (dz, dx, dy) != (0, 0, 0):
                pl.semaphore_signal(
                    barrier, inc=1, device_id=(zs[dz] * nx + xs[dx], ys[dy], blk), device_id_type=MESH
                )
    pl.semaphore_signal(barrier, inc=1, device_id=(gx, gy, 1 - blk), device_id_type=MESH)

    loads = [
        pltpu.make_async_copy(hull_hbm, HULL, in_sem.at[0]),
        pltpu.make_async_copy(p_hbm, E.at[pl.ds(3, X), pl.ds(8, Y)], in_sem.at[1]),
        pltpu.make_async_copy(b_hbm, EB.at[pl.ds(2, X), pl.ds(8, Y)], in_sem.at[2]),
        pltpu.make_async_copy(prev_hbm, PREV, in_sem.at[3]),
        pltpu.make_async_copy(kap_hbm, KAP, in_sem.at[4]),
    ]
    for load in loads:
        load.start()

    for ref, w in ((E, 3), (EB, 2), (E2, 3)):
        @pl.when(gx == 0)
        def _(ref=ref, w=w):
            ref[0:w] = jnp.zeros((w,) + ref.shape[1:], F32)

        @pl.when(gx == n_gx - 1)
        def _(ref=ref, w=w):
            ref[w + X :] = jnp.zeros((w,) + ref.shape[1:], F32)

        @pl.when(gy == 0)
        def _(ref=ref, w=w):
            ref[w : w + X, 0:8] = jnp.zeros((X, 8, LANES), F32)

        @pl.when(gy == ny - 1)
        def _(ref=ref, w=w):
            ref[w : w + X, 8 + Y :] = jnp.zeros((X, 8, LANES), F32)

    rb = rb_ref[...]
    owner = onehot(jnp.broadcast_to(rb, (NB, HR)) == lax.broadcasted_iota(jnp.int32, (NB, HR), 0))
    before = onehot(
        lax.broadcasted_iota(jnp.int32, (HR, HR), 0) < lax.broadcasted_iota(jnp.int32, (HR, HR), 1)
    )
    earlier = dot(owner, before)
    slot = jnp.sum(owner.astype(F32) * earlier, axis=0, keepdims=True).astype(jnp.int32)
    placing = rb * CAP + slot
    code = rc_ref[...] + 1
    lane_row = lax.broadcasted_iota(jnp.int32, (LANES, HR), 0)
    slot_b = jnp.broadcast_to(slot, (LANES, HR))
    picked_hi = jnp.where(lane_row == slot_b, jnp.broadcast_to(code // 32, (LANES, HR)), 0)
    picked_lo = jnp.where(lane_row == slot_b + CAP, jnp.broadcast_to(code % 32, (LANES, HR)), 0)
    codes = (picked_hi + picked_lo).astype(F32).astype(BF16)
    cols = dot_nt(owner, codes)
    SB[:, 8:16, :] = jnp.broadcast_to(cols.reshape(NB, 1, LANES), (NB, 8, LANES))

    loads[0].wait()
    hull_parts = parts(HULL[...])

    def pack(m, _):
        rows = lax.broadcasted_iota(jnp.int32, (GS, HR), 0) + m * GS
        pt = onehot(rows == jnp.broadcast_to(placing, (GS, HR)))
        SB[pl.ds(m * G, G), 0:8, :] = joined(dot(pt, hull_parts)).reshape(G, 8, LANES)
        return 0

    lax.fori_loop(0, nz, pack, 0)

    pl.semaphore_wait(barrier, NB)

    def shares(src, dst, width, lo, hi, send, recv):
        return [
            (gx < n_gx - 1, gx > 0, pltpu.make_async_remote_copy(
                src.at[pl.ds(X + lo - width, width), pl.ds(8, Y)], dst.at[pl.ds(lo - width, width), pl.ds(8, Y)],
                send.at[0], recv.at[0], device_id=(jnp.minimum(gx + 1, n_gx - 1), gy, blk), device_id_type=MESH)),
            (gx > 0, gx < n_gx - 1, pltpu.make_async_remote_copy(
                src.at[pl.ds(lo, width), pl.ds(8, Y)], dst.at[pl.ds(X + lo, width), pl.ds(8, Y)],
                send.at[1], recv.at[1], device_id=(jnp.maximum(gx - 1, 0), gy, blk), device_id_type=MESH)),
            (gy < ny - 1, gy > 0, pltpu.make_async_remote_copy(
                src.at[pl.ds(lo, X), pl.ds(Y, 8)], dst.at[pl.ds(lo, X), pl.ds(0, 8)],
                send.at[2], recv.at[2], device_id=(gx, jnp.minimum(gy + 1, ny - 1), blk), device_id_type=MESH)),
            (gy > 0, gy < ny - 1, pltpu.make_async_remote_copy(
                src.at[pl.ds(lo, X), pl.ds(8, 8)], dst.at[pl.ds(lo, X), pl.ds(8 + Y, 8)],
                send.at[3], recv.at[3], device_id=(gx, jnp.maximum(gy - 1, 0), blk), device_id_type=MESH)),
            (None, None, pltpu.make_async_remote_copy(
                src.at[pl.ds(lo, X), pl.ds(8, Y)], hi,
                send.at[4], recv.at[4], device_id=(gx, gy, 1 - blk), device_id_type=MESH)),
        ]

    def start(copies):
        for sends, _, copy in copies:
            if sends is None:
                copy.start()
            else:
                pl.when(sends)(lambda copy=copy: copy.start())

    def finish(copies):
        for sends, gets, copy in copies:
            if sends is None:
                copy.wait_send()
                copy.wait_recv()
            else:
                pl.when(sends)(lambda copy=copy: copy.wait_send())
                pl.when(gets)(lambda copy=copy: copy.wait_recv())

    loads[1].wait()
    loads[2].wait()
    halo_p = shares(E, E, 3, 3, OP, hs_sem.at[0], hr_sem.at[0])
    halo_b = shares(EB, EB, 2, 2, OB, hs_sem.at[1], hr_sem.at[1])
    start(halo_p)
    start(halo_b)

    for dz in order:
        for dx, dy in offsets[dz]:
            k = (dz * nx + dx) * ny + dy
            if k == 0:
                continue
            dest_gx = zs[dz] * nx + xs[dx]
            pltpu.make_async_remote_copy(
                SB.at[dest_gx * ny + ys[dy], pl.ds(0, MSG)], RV.at[k, pl.ds(0, MSG)],
                as_sem, ar_sem.at[dz], device_id=(dest_gx, ys[dy], blk), device_id_type=MESH,
            ).start()
    own = pltpu.make_async_copy(SB.at[me, pl.ds(0, MSG)], RV.at[0, pl.ds(0, MSG)], self_sem.at[0])
    own.start()

    weights_row = lax.broadcasted_iota(jnp.int32, (16, LANES), 0)
    place_row = lax.broadcasted_iota(jnp.int32, (16, HR), 0)
    place_code = jnp.where(
        place_row == 0, jnp.broadcast_to(placing // 32, (16, HR)),
        jnp.where(place_row == 1, jnp.broadcast_to(placing % 32, (16, HR)), 0),
    ).astype(F32).astype(BF16)
    place_w = jnp.where(weights_row == 0, 32.0, jnp.where(weights_row == 1, 1.0, 0.0)).astype(BF16)
    placing_col = dot_tn(place_code, place_w)
    span = min(LANES, NB * CAP)
    for m in range(NB * CAP // span):
        cell = (lax.broadcasted_iota(jnp.int32, (HR, span), 1) + m * span).astype(F32)
        PM[:, m * span : (m + 1) * span] = onehot(placing_col[:, :span] == cell)

    lane = lax.broadcasted_iota(jnp.int32, (Y, LANES), 1)
    mine_left = jnp.broadcast_to(blk, (Y, LANES)) == 0
    halo_lanes = (lane < LANES // 2) == mine_left

    def outer(other):
        return jnp.where(halo_lanes, other, 0.0)

    def up(k, near, far):
        return pltpu.roll(jnp.where(lane < k, far, near), LANES - k, 1)

    def down(k, near, far):
        return pltpu.roll(jnp.where(lane >= LANES - k, far, near), k, 1)

    finish(halo_b)

    def faces_x(i, _):
        BX[i] = (EB[i, 8 : 8 + Y] + EB[i + 1, 8 : 8 + Y]) * FACE
        return 0

    lax.fori_loop(0, X + 3, faces_x, 0)

    def faces_yz(i, _):
        BY[i] = (EB[i + 2, 6 : 14 + Y] + EB[i + 2, 7 : 15 + Y]) * FACE
        own_b = EB[i + 2, 8 : 8 + Y]
        far_b = outer(OB[i])
        BZ[i] = (own_b + up(1, own_b, far_b)) * FACE
        BZO[i] = (far_b + up(1, far_b, own_b)) * FACE
        return 0

    lax.fori_loop(0, X, faces_yz, 0)

    def flux_x(src):
        def body(i, _):
            FX[i] = wide(src[i, 8 : 8 + Y], src[i + 1, 8 : 8 + Y], src[i + 2, 8 : 8 + Y], src[i + 3, 8 : 8 + Y]) * BX[i]
            return 0

        lax.fori_loop(0, X + 3, body, 0)

    def laplace(src, other, i):
        total = wide(FX[i], FX[i + 1], FX[i + 2], FX[i + 3])
        FY[...] = wide(src[i + 3, 5 : 13 + Y], src[i + 3, 6 : 14 + Y], src[i + 3, 7 : 15 + Y], src[i + 3, 8 : 16 + Y]) * BY[i]
        total = total + wide(FY[0:Y], FY[1 : 1 + Y], FY[2 : 2 + Y], FY[3 : 3 + Y])
        near = src[i + 3, 8 : 8 + Y]
        far = outer(other[i])
        flux = wide(down(1, near, far), near, up(1, near, far), up(2, near, far)) * BZ[i]
        beyond = wide(down(1, far, near), far, up(1, far, near), up(2, far, near)) * BZO[i]
        return total + wide(down(2, flux, beyond), down(1, flux, beyond), flux, up(1, flux, beyond))

    loads[3].wait()
    loads[4].wait()
    finish(halo_p)
    flux_x(E)

    def first(i, _):
        E2[i + 3, 8 : 8 + Y] = 2.0 * E[i + 3, 8 : 8 + Y] - PREV[i] + KAP[i] * laplace(E, OP, i)
        return 0

    lax.fori_loop(0, X, first, 0)

    def wait_group(buf, rows, count, sem):
        ref = buf.at[pl.ds(0, count), pl.ds(0, rows)]
        pltpu.make_async_copy(ref, ref, sem).wait()

    tag = lax.broadcasted_iota(jnp.int32, (8, LANES), 1)
    row8 = lax.broadcasted_iota(jnp.int32, (8, LANES), 0)
    keep = (tag == row8) | (tag == row8 + CAP)
    w_lane = lax.broadcasted_iota(jnp.int32, (8, LANES), 1)
    w_code = jnp.where(w_lane < CAP, 32.0, jnp.where(w_lane < 2 * CAP, 1.0, 0.0)).astype(BF16)
    cells = X * Y

    def masked(dz):
        rows = [
            jnp.where(keep, jnp.broadcast_to(RV[dz * G + j, 8:9, :], (8, LANES)), 0.0) for j in range(G)
        ]
        return jnp.concatenate(rows, axis=0).astype(BF16)

    chunk = min(256, cells)
    for n, dz in enumerate(order):
        if dz == 0:
            if G > 1:
                wait_group(RV, MSG, G - 1, ar_sem.at[0])
            own.wait()
        else:
            wait_group(RV, MSG, G, ar_sem.at[dz])
        col_lane = dot_nt(w_code, masked(dz)).astype(jnp.int32) - 1
        rows = parts(RV[dz * G : (dz + 1) * G, 0:8, :].reshape(GS, LANES))
        col_b = jnp.broadcast_to(col_lane[0:1], (chunk, GS))

        def add(m, _, first_group=(n == 0), rows=rows, col_b=col_b):
            ids = lax.broadcasted_iota(jnp.int32, (chunk, GS), 0) + m * chunk
            val = joined(dot(onehot(ids == col_b), rows))
            at = pl.ds(m * chunk, chunk)
            SRC[at] = val if first_group else SRC[at] + val
            return 0

        lax.fori_loop(0, cells // chunk, add, 0)

    def middle(i, _):
        pushed = (GAIN * KAP[i]) * SRC[pl.ds(i * Y, Y)]
        E2[i + 3, 8 : 8 + Y] = E2[i + 3, 8 : 8 + Y] + pushed
        PREV[i] = pushed - E[i + 3, 8 : 8 + Y]
        return 0

    lax.fori_loop(0, X, middle, 0)
    halo_m = shares(E2, E2, 3, 3, OM, ms_sem, mr_sem)
    start(halo_m)

    w_full = jnp.where(
        lax.broadcasted_iota(jnp.int32, (LANES, LANES), 0) < CAP, 32.0,
        jnp.where(lax.broadcasted_iota(jnp.int32, (LANES, LANES), 0) < 2 * CAP, 1.0, 0.0),
    ).astype(BF16)
    for dz in order:
        col_sub = dot(masked(dz), w_full) - 1.0

        for m in range(cells // LANES):
            ids = (lax.broadcasted_iota(jnp.int32, (GS, LANES), 1) + m * LANES).astype(F32)
            Q[dz * GS : (dz + 1) * GS, m * LANES : (m + 1) * LANES] = onehot(col_sub == ids)

    finish(halo_m)
    flux_x(E2)

    def second(i, _):
        val = 2.0 * E2[i + 3, 8 : 8 + Y] + PREV[i] + KAP[i] * laplace(E2, OM, i)
        OP[i] = val
        hi, lo = split2(val)
        NEXT[pl.ds(i * Y, Y), 0:LANES] = hi
        NEXT[pl.ds(i * Y, Y), LANES : 2 * LANES] = lo
        return 0

    lax.fori_loop(0, X, second, 0)
    out_copy = pltpu.make_async_copy(OP, out_hbm, out_sem.at[0])
    out_copy.start()

    for dz in order:
        PK[dz * G : (dz + 1) * G] = joined(dot(Q[dz * GS : (dz + 1) * GS], NEXT[...])).reshape(G, 8, LANES)
        for dx, dy in offsets[dz]:
            k = (dz * nx + dx) * ny + dy
            if k == 0:
                continue
            pltpu.make_async_remote_copy(
                PK.at[k], RET.at[me], bs_sem, br_sem,
                device_id=(zb[dz] * nx + xb[dx], yb[dy], blk), device_id_type=MESH,
            ).start()
    back = pltpu.make_async_copy(PK.at[0], RET.at[me], self_sem.at[1])
    back.start()

    sent = SB.at[pl.ds(0, NB - 1), pl.ds(0, MSG)]
    pltpu.make_async_copy(sent, sent, as_sem).wait()
    for sem in (bs_sem, br_sem):
        moved = PK.at[pl.ds(0, NB - 1)]
        pltpu.make_async_copy(moved, moved, sem).wait()
    back.wait()
    HOUT[...] = joined(dot(PM[...], parts(RET[...].reshape(NB * CAP, LANES))))
    hull_copy = pltpu.make_async_copy(HOUT, hp_hbm, out_sem.at[1])
    hull_copy.start()
    hull_copy.wait()
    out_copy.wait()


def solution(mesh):
    n_gx, n_gy = mesh.shape["gx"], mesh.shape["gy"]
    dims = torus(n_gx, n_gy)
    NB = n_gx * n_gy

    def local(pressure, pressure_prev, buoyancy, kappa, hull_accel, row_block, row_column):
        X, Y, Z = pressure.shape
        HR = hull_accel.shape[0]
        any_spec = pl.BlockSpec(memory_space=pl.ANY)
        vmem_spec = pl.BlockSpec(memory_space=pltpu.VMEM)
        dma = pltpu.SemaphoreType.DMA
        V = pltpu.VMEM
        return pl.pallas_call(
            functools.partial(kernel, dims),
            out_shape=(
                jax.ShapeDtypeStruct((X, Y, Z), F32),
                jax.ShapeDtypeStruct((HR, Z), F32),
            ),
            in_specs=[any_spec] * 5 + [vmem_spec] * 2,
            out_specs=[any_spec] * 2,
            scratch_shapes=[
                V((X + 6, Y + 16, Z), F32),
                V((X + 4, Y + 16, Z), F32),
                V((X + 6, Y + 16, Z), F32),
                V((X, Y, Z), F32),
                V((X, Y, Z), F32),
                V((X, Y, Z), F32),
                V((X, Y, Z), F32),
                V((X, Y, Z), F32),
                V((HR, Z), F32),
                V((X + 3, Y, Z), F32),
                V((Y + 8, Z), F32),
                V((X + 3, Y, Z), F32),
                V((X, Y + 8, Z), F32),
                V((X, Y, Z), F32),
                V((X, Y, Z), F32),
                V((X * Y, Z), F32),
                V((X * Y, 2 * Z), BF16),
                V((NB, 16, Z), F32),
                V((NB, 16, Z), F32),
                V((NB, CAP, Z), F32),
                V((NB, CAP, Z), F32),
                V((NB * CAP, X * Y), BF16),
                V((HR, NB * CAP), BF16),
                V((HR, Z), F32),
                dma((5,)), dma((2,)), dma((2, 5)), dma((2, 5)), dma((5,)), dma((5,)),
                dma, dma((dims[0],)), dma, dma, dma((2,)),
            ],
            compiler_params=pltpu.CompilerParams(collective_id=0, has_side_effects=True, vmem_limit_bytes=60 * 1024 * 1024),
            name="hull_leapfrog",
        )(
            pressure, pressure_prev, buoyancy, kappa, hull_accel,
            row_block.reshape(1, HR), row_column.reshape(1, HR),
        )

    return jax.shard_map(
        local,
        mesh=mesh,
        in_specs=(
            P("gx", "gy", "blk"),
            P("gx", "gy", "blk"),
            P("gx", "gy", "blk"),
            P("gx", "gy", "blk"),
            P(("gx", "gy", "blk"), None),
            P(("gx", "gy", "blk"), None),
            P(("gx", "gy", "blk"), None),
        ),
        out_specs=(P("gx", "gy", "blk"), P(("gx", "gy", "blk"), None)),
        check_vma=False,
    )
```

profile of v0, /device:TPU:1, one launch (start us, length us, event | category | flops | bytes accessed | tf_op | source)
XLA Modules:
  0.0 64.3 jit_solution(12964225684711309830)
XLA Ops:
  0.6 61.0 %hull_leapfrog.1 = (f32[16,64,128]{2,1,0:T(8,128)}, f32[512,128]{1,0:T(8,128)}) custom-call(f32[16,64,128]{2,1,0:T(8,128)} %p_hbm.1, f32[16,64,128]{2,1,0:T(8,128)} %prev_hbm.1, f32[16,64,128]{2,1,0:T(8,128)} %b_hbm.1, f32[16,64,128]{2,1,0:T(8,128)} %kap_hbm.1, f32[512,128]{1,0:T(8,128)} %hull_hbm.1, s32[1,512]{1,0:T(1,128)} %bitcast.2, s32[1,512]{1,0:T(1,128)} %bitcast.3), custom_call_target="tpu_custom_call" | custom-call | tf_op jit(solution)/shard_map/hull_leapfrog/pallas_call | solution.py:401
  61.7 0.0 copy-start
  61.7 1.9 %copy.11 = f32[16,64,128]{2,1,0:T(8,128)} copy(f32[16,64,128]{2,1,0:T(8,128)} %get-tuple-element.4) | data formatting | bytes 1048576
  63.6 0.0 copy-done
  63.6 0.7 %copy.12 = f32[512,128]{1,0:T(8,128)} copy(f32[512,128]{1,0:T(8,128)S(1)} %copy-done) | data formatting | bytes 524288
Async XLA Ops:
  61.7 1.9 %copy-start = (f32[512,128]{1,0:T(8,128)S(1)}, f32[512,128]{1,0:T(8,128)}, u32[]{:S(2)}) copy-start(f32[512,128]{1,0:T(8,128)} %get-tuple-element.5) | copy-start | bytes 786436
where the time goes:
time: 64.5 us; the launch traced here: 64.3 us
  Pallas kernels  61 us (95%)
  local copies, waits for them, and re-layouts  2.63 us (4%)
  between operations  0.65 us (1%)
    pallas_call x1, Pallas kernels, local(): pl.pallas_call(functools.partial(kernel, dims), out_shape=(jax.ShapeDtype...  61 us
    unnamed x4, local copies, waits for them, and re-layouts  2.63 us

commit v1 on v0

v1 whole, which is shorter than its diff:
```python
import functools

import jax
import jax.numpy as jnp
from jax import lax
from jax.experimental import pallas as pl
from jax.experimental.pallas import tpu as pltpu
from jax.sharding import PartitionSpec as P

MESH = pl.DeviceIdType.MESH
F32 = jnp.float32
BF16 = jnp.bfloat16
LANES = 128
CAP = 8
COURANT = 0.05
GAIN = 0.5
FACE = COURANT * 0.5 / 576.0


def torus(n_gx, n_gy):
    nx = 4 if n_gx % 4 == 0 and n_gx > 4 else 2
    return n_gx // nx, nx, n_gy


def split2(v):
    hi = v.astype(BF16)
    lo = (v - hi.astype(F32)).astype(BF16)
    return hi, lo


def parts(v):
    hi, lo = split2(v)
    return jnp.concatenate([hi, lo], axis=1)


def joined(v):
    return v[:, :LANES] + v[:, LANES:]


def wide(a, b, c, d):
    return 27.0 * (c - b) - (d - a)


def dot(a, b):
    return jnp.dot(a, b, preferred_element_type=F32)


def dot_nt(a, b):
    return lax.dot_general(a, b, (((1,), (1,)), ((), ())), preferred_element_type=F32)


def dot_tn(a, b):
    return lax.dot_general(a, b, (((0,), (0,)), ((), ())), preferred_element_type=F32)


def onehot(mask):
    return jnp.where(mask, 1.0, 0.0).astype(BF16)


def kernel(
    dims,
    p_hbm, prev_hbm, b_hbm, kap_hbm, hull_hbm, rb_ref, rc_ref,
    out_hbm, hp_hbm,
    E, EB, E2, ZS, ZR, PREV, KAP, HULL, FX, FY, TOT, BX, BY, BZ, BZO, NEXT,
    CS, CR, CA, MC, SB, RV, PK, RET, Q, QT, PM, HOUT,
    in_sem, out_sem, hs_sem, hr_sem, cs_sem, cr_sem, fs_sem, fr_sem, as_sem, ar_sem, bs_sem, br_sem, self_sem,
):
    nz, nx, ny = dims
    NB = nz * nx * ny
    G = nx * ny
    GS = G * CAP
    X, Y = PREV.shape[0], PREV.shape[1]
    T = Y // 8
    PER = LANES // (4 * T)
    HR = HULL.shape[0]
    cells = X * Y
    n_gx = nz * nx
    gx = lax.axis_index("gx")
    gy = lax.axis_index("gy")
    blk = lax.axis_index("blk")
    zi = gx // nx
    xi = gx % nx
    me = gx * ny + gy
    spot = xi * ny + gy

    zs = [(zi + dz) % nz for dz in range(nz)]
    xs = [(xi + dx) % nx for dx in range(nx)]
    ys = [(gy + dy) % ny for dy in range(ny)]
    zb = [(zi + nz - dz) % nz for dz in range(nz)]
    xb = [(xi + nx - dx) % nx for dx in range(nx)]
    yb = [(gy + ny - dy) % ny for dy in range(ny)]
    half = nz // 2
    order = [half]
    for step in range(half - 1, 0, -1):
        order += [step, nz - step]
    order += [0]
    plane = [(dx, dy) for dx in range(nx) for dy in range(ny)]

    barrier = pltpu.get_barrier_semaphore()
    for dz in order:
        for dx, dy in plane:
            if (dz, dx, dy) != (0, 0, 0):
                pl.semaphore_signal(
                    barrier, inc=1, device_id=(zs[dz] * nx + xs[dx], ys[dy], blk), device_id_type=MESH
                )
    pl.semaphore_signal(barrier, inc=1, device_id=(gx, gy, 1 - blk), device_id_type=MESH)

    loads = [
        pltpu.make_async_copy(hull_hbm, HULL, in_sem.at[0]),
        pltpu.make_async_copy(p_hbm, E.at[pl.ds(3, X), pl.ds(8, Y)], in_sem.at[1]),
        pltpu.make_async_copy(b_hbm, EB.at[pl.ds(2, X), pl.ds(8, Y)], in_sem.at[2]),
        pltpu.make_async_copy(prev_hbm, PREV, in_sem.at[3]),
        pltpu.make_async_copy(kap_hbm, KAP, in_sem.at[4]),
    ]
    for load in loads:
        load.start()

    for ref, w in ((E, 3), (EB, 2), (E2, 3)):
        @pl.when(gx == 0)
        def _(ref=ref, w=w):
            ref[0:w] = jnp.zeros((w,) + ref.shape[1:], F32)

        @pl.when(gx == n_gx - 1)
        def _(ref=ref, w=w):
            ref[w + X :] = jnp.zeros((w,) + ref.shape[1:], F32)

        @pl.when(gy == 0)
        def _(ref=ref, w=w):
            ref[w : w + X, 0:8] = jnp.zeros((X, 8, LANES), F32)

        @pl.when(gy == ny - 1)
        def _(ref=ref, w=w):
            ref[w : w + X, 8 + Y :] = jnp.zeros((X, 8, LANES), F32)

    rb = rb_ref[...]
    owner = onehot(jnp.broadcast_to(rb, (NB, HR)) == lax.broadcasted_iota(jnp.int32, (NB, HR), 0))
    before = onehot(
        lax.broadcasted_iota(jnp.int32, (HR, HR), 0) < lax.broadcasted_iota(jnp.int32, (HR, HR), 1)
    )
    earlier = dot(owner, before)
    slot = jnp.sum(owner.astype(F32) * earlier, axis=0, keepdims=True).astype(jnp.int32)
    placing = rb * CAP + slot
    code = rc_ref[...] + 1
    row_z = lax.broadcasted_iota(jnp.int32, (16, HR), 0)
    which_z = jnp.broadcast_to(placing // GS, (16, HR))
    coded = jnp.where(row_z == which_z, jnp.broadcast_to(code // 32, (16, HR)), 0) + jnp.where(
        row_z == which_z + 8, jnp.broadcast_to(code % 32, (16, HR)), 0
    )
    lane_of = onehot(lax.broadcasted_iota(jnp.int32, (LANES, HR), 0) == jnp.broadcast_to(placing % GS, (LANES, HR)))
    sums = dot_nt(coded.astype(F32).astype(BF16), lane_of)
    CS[...] = sums[0:8] * 32.0 + sums[8:16]

    loads[0].wait()
    hull_parts = parts(HULL[...])

    def pack(m, _):
        rows = lax.broadcasted_iota(jnp.int32, (GS, HR), 0) + m * GS
        pt = onehot(rows == jnp.broadcast_to(placing, (GS, HR)))
        SB[pl.ds(m * G, G)] = joined(dot(pt, hull_parts)).reshape(G, 8, LANES)
        return 0

    lax.fori_loop(0, nz, pack, 0)

    lane8 = lax.broadcasted_iota(jnp.int32, (8, LANES), 1)
    edge = jnp.where(jnp.broadcast_to(blk, (8, LANES)) == 0, (lane8 + 3) % LANES, lane8) // 4

    def gather_edge(field, ref, lo):
        for q in range(X // PER):
            acc = jnp.zeros((8, LANES), F32)
            for i in range(PER):
                for t in range(T):
                    m = i * T + t
                    tile = ref[lo + q * PER + i, 8 + 8 * t : 16 + 8 * t]
                    acc = jnp.where(edge == m, pltpu.roll(tile, 4 * m, 1) if m else tile, acc)
            ZS[field, q] = acc

    loads[1].wait()
    loads[2].wait()
    gather_edge(0, E, 3)
    gather_edge(1, EB, 2)

    pl.semaphore_wait(barrier, NB)

    def shares(ref, field, width):
        lo = width
        send, recv = hs_sem.at[field], hr_sem.at[field]
        return [
            (gx < n_gx - 1, gx > 0, pltpu.make_async_remote_copy(
                ref.at[pl.ds(X + lo - width, width), pl.ds(8, Y)], ref.at[pl.ds(lo - width, width), pl.ds(8, Y)],
                send.at[0], recv.at[0], device_id=(jnp.minimum(gx + 1, n_gx - 1), gy, blk), device_id_type=MESH)),
            (gx > 0, gx < n_gx - 1, pltpu.make_async_remote_copy(
                ref.at[pl.ds(lo, width), pl.ds(8, Y)], ref.at[pl.ds(X + lo, width), pl.ds(8, Y)],
                send.at[1], recv.at[1], device_id=(jnp.maximum(gx - 1, 0), gy, blk), device_id_type=MESH)),
            (gy < ny - 1, gy > 0, pltpu.make_async_remote_copy(
                ref.at[pl.ds(lo, X), pl.ds(Y, 8)], ref.at[pl.ds(lo, X), pl.ds(0, 8)],
                send.at[2], recv.at[2], device_id=(gx, jnp.minimum(gy + 1, ny - 1), blk), device_id_type=MESH)),
            (gy > 0, gy < ny - 1, pltpu.make_async_remote_copy(
                ref.at[pl.ds(lo, X), pl.ds(8, 8)], ref.at[pl.ds(lo, X), pl.ds(8 + Y, 8)],
                send.at[3], recv.at[3], device_id=(gx, jnp.maximum(gy - 1, 0), blk), device_id_type=MESH)),
            (None, None, pltpu.make_async_remote_copy(
                ZS.at[field], ZR.at[field],
                send.at[4], recv.at[4], device_id=(gx, gy, 1 - blk), device_id_type=MESH)),
        ]

    def start(copies):
        for sends, _, copy in copies:
            if sends is None:
                copy.start()
            else:
                pl.when(sends)(lambda copy=copy: copy.start())

    def finish(copies):
        for sends, gets, copy in copies:
            if sends is None:
                copy.wait_send()
                copy.wait_recv()
            else:
                pl.when(sends)(lambda copy=copy: copy.wait_send())
                pl.when(gets)(lambda copy=copy: copy.wait_recv())

    def drained(ref, sem):
        pltpu.make_async_copy(ref, ref, sem).wait()

    for dz in range(1, nz):
        pltpu.make_async_remote_copy(
            CS.at[pl.ds(zs[dz], 1)], CR.at[pl.ds(dz, 1)], cs_sem, cr_sem,
            device_id=(zs[dz] * nx + xi, gy, blk), device_id_type=MESH,
        ).start()
    own_col = pltpu.make_async_copy(CS.at[pl.ds(zi, 1)], CR.at[pl.ds(0, 1)], self_sem.at[0])
    own_col.start()

    halo_p = shares(E, 0, 3)
    halo_b = shares(EB, 1, 2)
    start(halo_p)
    start(halo_b)

    for dz in order:
        for dx, dy in plane:
            k = (dz * nx + dx) * ny + dy
            if k == 0:
                continue
            dest_gx = zs[dz] * nx + xs[dx]
            pltpu.make_async_remote_copy(
                SB.at[dest_gx * ny + ys[dy]], RV.at[k], as_sem, ar_sem,
                device_id=(dest_gx, ys[dy], blk), device_id_type=MESH,
            ).start()
    own = pltpu.make_async_copy(SB.at[me], RV.at[0], self_sem.at[1])
    own.start()

    drained(CR.at[pl.ds(0, nz - 1)], cr_sem)
    own_col.wait()
    for dx, dy in plane[1:]:
        pltpu.make_async_remote_copy(
            CR, CA.at[dx * ny + dy], fs_sem, fr_sem,
            device_id=(zi * nx + xs[dx], ys[dy], blk), device_id_type=MESH,
        ).start()
    own_tile = pltpu.make_async_copy(CR, CA.at[0], self_sem.at[2])
    own_tile.start()

    weights_row = lax.broadcasted_iota(jnp.int32, (16, LANES), 0)
    place_row = lax.broadcasted_iota(jnp.int32, (16, HR), 0)
    place_code = jnp.where(
        place_row == 0, jnp.broadcast_to(placing // 32, (16, HR)),
        jnp.where(place_row == 1, jnp.broadcast_to(placing % 32, (16, HR)), 0),
    ).astype(F32).astype(BF16)
    place_w = jnp.where(weights_row == 0, 32.0, jnp.where(weights_row == 1, 1.0, 0.0)).astype(BF16)
    placing_col = dot_tn(place_code, place_w)
    span = min(LANES, NB * CAP)
    for m in range(NB * CAP // span):
        cell = (lax.broadcasted_iota(jnp.int32, (HR, span), 1) + m * span).astype(F32)
        PM[:, m * span : (m + 1) * span] = onehot(placing_col[:, :span] == cell)

    lane = lax.broadcasted_iota(jnp.int32, (Y, LANES), 1)
    halo_lanes = (lane < LANES // 2) == (jnp.broadcast_to(blk, (Y, LANES)) == 0)

    def beside(field, q, i):
        packed = ZR[field, q]
        tiles = []
        for t in range(T):
            m = i * T + t
            tiles.append(pltpu.roll(packed, LANES - 4 * m, 1) if m else packed)
        return jnp.where(halo_lanes, jnp.concatenate(tiles, axis=0), 0.0)

    def up(k, near, far):
        return pltpu.roll(jnp.where(lane < k, far, near), LANES - k, 1)

    def down(k, near, far):
        return pltpu.roll(jnp.where(lane >= LANES - k, far, near), k, 1)

    finish(halo_b)

    def faces(q, _):
        for i in range(PER):
            c = q * PER + i
            BX[c] = (EB[c, 8 : 8 + Y] + EB[c + 1, 8 : 8 + Y]) * FACE
            BY[c] = (EB[c + 2, 6 : 14 + Y] + EB[c + 2, 7 : 15 + Y]) * FACE
            own_b = EB[c + 2, 8 : 8 + Y]
            far_b = beside(1, q, i)
            BZ[c] = (own_b + up(1, own_b, far_b)) * FACE
            BZO[c] = (far_b + up(1, far_b, own_b)) * FACE
        return 0

    lax.fori_loop(0, X // PER, faces, 0)
    for c in range(X, X + 3):
        BX[c] = (EB[c, 8 : 8 + Y] + EB[c + 1, 8 : 8 + Y]) * FACE

    def flux_x(src, c):
        FX[c] = wide(src[c, 8 : 8 + Y], src[c + 1, 8 : 8 + Y], src[c + 2, 8 : 8 + Y], src[c + 3, 8 : 8 + Y]) * BX[c]

    def inner_x(src):
        for c in range(3, X):
            flux_x(src, c)

    def outer_x(src):
        for c in (0, 1, 2, X, X + 1, X + 2):
            flux_x(src, c)

    def across(src, field):
        def body(q, _):
            for i in range(PER):
                c = q * PER + i
                FY[i] = wide(src[c + 3, 5 : 13 + Y], src[c + 3, 6 : 14 + Y], src[c + 3, 7 : 15 + Y], src[c + 3, 8 : 16 + Y]) * BY[c]
                near = src[c + 3, 8 : 8 + Y]
                far = beside(field, q, i)
                flux = wide(down(1, near, far), near, up(1, near, far), up(2, near, far)) * BZ[c]
                beyond = wide(down(1, far, near), far, up(1, far, near), up(2, far, near)) * BZO[c]
                TOT[c] = wide(FY[i, 0:Y], FY[i, 1 : 1 + Y], FY[i, 2 : 2 + Y], FY[i, 3 : 3 + Y]) + wide(
                    down(2, flux, beyond), down(1, flux, beyond), flux, up(1, flux, beyond)
                )
            return 0

        lax.fori_loop(0, X // PER, body, 0)

    def laplace(c):
        return TOT[c] + wide(FX[c], FX[c + 1], FX[c + 2], FX[c + 3])

    loads[3].wait()
    loads[4].wait()
    finish(halo_p)
    inner_x(E)
    outer_x(E)
    across(E, 0)

    def first(q, _):
        for i in range(PER):
            c = q * PER + i
            E2[c + 3, 8 : 8 + Y] = 2.0 * E[c + 3, 8 : 8 + Y] - PREV[c] + KAP[c] * laplace(c)
        return 0

    lax.fori_loop(0, X // PER, first, 0)

    drained(CA.at[pl.ds(0, G - 1)], fr_sem)
    own_tile.wait()
    keep = lane8 == lax.broadcasted_iota(jnp.int32, (8, LANES), 0) + spot * CAP
    for dz in range(nz):
        for j in range(G):
            line = jnp.where(keep, jnp.broadcast_to(CA[j, dz : dz + 1, :], (8, LANES)), 0.0)
            high = jnp.floor(line * (1.0 / 32.0))
            at = (dz * G + j) * 8
            MC[at : at + 8, 0:LANES] = high
            MC[at : at + 8, LANES:] = line - 32.0 * high
    w_lane = jnp.where(lax.broadcasted_iota(jnp.int32, (8, 2 * LANES), 1) < LANES, 32.0, 1.0).astype(BF16)
    w_full = jnp.where(lax.broadcasted_iota(jnp.int32, (2 * LANES, LANES), 0) < LANES, 32.0, 1.0).astype(BF16)
    col_lane = dot_nt(w_lane, MC[...].astype(BF16))[0:1].astype(jnp.int32) - 1
    chunk = min(LANES, cells)

    def build_qt(m, _):
        ids = lax.broadcasted_iota(jnp.int32, (chunk, NB * CAP), 0) + m * chunk
        QT[pl.ds(m * chunk, chunk)] = onehot(ids == jnp.broadcast_to(col_lane, (chunk, NB * CAP)))
        return 0

    lax.fori_loop(0, cells // chunk, build_qt, 0)

    def build_q(dz, _):
        col_sub = dot(MC[pl.ds(dz * GS, GS)].astype(BF16), w_full) - 1.0
        for m in range(cells // chunk):
            ids = (lax.broadcasted_iota(jnp.int32, (GS, chunk), 1) + m * chunk).astype(F32)
            Q[pl.ds(dz * GS, GS), m * chunk : (m + 1) * chunk] = onehot(col_sub[:, :chunk] == ids)
        return 0

    lax.fori_loop(0, nz, build_q, 0)

    drained(RV.at[pl.ds(0, NB - 1)], ar_sem)
    own.wait()
    rows = parts(RV[...].reshape(NB * CAP, LANES))
    halo_m = shares(E2, 2, 3)

    def middle(q, _):
        pushed = joined(dot(QT[pl.ds(q * PER * Y, PER * Y)], rows)).reshape(PER, Y, LANES)
        for i in range(PER):
            c = q * PER + i
            force = (GAIN * KAP[c]) * pushed[i]
            E2[c + 3, 8 : 8 + Y] = E2[c + 3, 8 : 8 + Y] + force
            PREV[c] = force - E[c + 3, 8 : 8 + Y]
        return 0

    lax.fori_loop(0, X // PER, middle, 0)
    start(halo_m[0:4])
    gather_edge(2, E2, 3)
    start(halo_m[4:5])
    inner_x(E2)
    finish(halo_m[4:5])
    finish(halo_m[2:4])
    across(E2, 2)
    finish(halo_m[0:2])
    outer_x(E2)

    def second(q, _):
        for i in range(PER):
            c = q * PER + i
            val = 2.0 * E2[c + 3, 8 : 8 + Y] + PREV[c] + KAP[c] * laplace(c)
            TOT[c] = val
            hi, lo = split2(val)
            NEXT[pl.ds(c * Y, Y), 0:LANES] = hi
            NEXT[pl.ds(c * Y, Y), LANES : 2 * LANES] = lo
        return 0

    lax.fori_loop(0, X // PER, second, 0)
    out_copy = pltpu.make_async_copy(TOT, out_hbm, out_sem.at[0])
    out_copy.start()

    for dz in order:
        PK[dz * G : (dz + 1) * G] = joined(dot(Q[dz * GS : (dz + 1) * GS], NEXT[...])).reshape(G, 8, LANES)
        for dx, dy in plane:
            k = (dz * nx + dx) * ny + dy
            if k == 0:
                continue
            pltpu.make_async_remote_copy(
                PK.at[k], RET.at[me], bs_sem, br_sem,
                device_id=(zb[dz] * nx + xb[dx], yb[dy], blk), device_id_type=MESH,
            ).start()
    back = pltpu.make_async_copy(PK.at[0], RET.at[me], self_sem.at[3])
    back.start()

    drained(CR.at[pl.ds(0, nz - 1)], cs_sem)
    drained(CA.at[pl.ds(0, G - 1)], fs_sem)
    drained(SB.at[pl.ds(0, NB - 1)], as_sem)
    drained(PK.at[pl.ds(0, NB - 1)], bs_sem)
    drained(RET.at[pl.ds(0, NB - 1)], br_sem)
    back.wait()
    HOUT[...] = joined(dot(PM[...], parts(RET[...].reshape(NB * CAP, LANES))))
    hull_copy = pltpu.make_async_copy(HOUT, hp_hbm, out_sem.at[1])
    hull_copy.start()
    hull_copy.wait()
    out_copy.wait()


def solution(mesh):
    n_gx, n_gy = mesh.shape["gx"], mesh.shape["gy"]
    dims = torus(n_gx, n_gy)
    NB = n_gx * n_gy

    def local(pressure, pressure_prev, buoyancy, kappa, hull_accel, row_block, row_column):
        X, Y, Z = pressure.shape
        HR = hull_accel.shape[0]
        any_spec = pl.BlockSpec(memory_space=pl.ANY)
        vmem_spec = pl.BlockSpec(memory_space=pltpu.VMEM)
        dma = pltpu.SemaphoreType.DMA
        V = pltpu.VMEM
        return pl.pallas_call(
            functools.partial(kernel, dims),
            out_shape=(
                jax.ShapeDtypeStruct((X, Y, Z), F32),
                jax.ShapeDtypeStruct((HR, Z), F32),
            ),
            in_specs=[any_spec] * 5 + [vmem_spec] * 2,
            out_specs=[any_spec] * 2,
            scratch_shapes=[
                V((X + 6, Y + 16, Z), F32),
                V((X + 4, Y + 16, Z), F32),
                V((X + 6, Y + 16, Z), F32),
                V((3, X * Y // 256, 8, Z), F32),
                V((3, X * Y // 256, 8, Z), F32),
                V((X, Y, Z), F32),
                V((X, Y, Z), F32),
                V((HR, Z), F32),
                V((X + 3, Y, Z), F32),
                V((256 // Y, Y + 8, Z), F32),
                V((X, Y, Z), F32),
                V((X + 3, Y, Z), F32),
                V((X, Y + 8, Z), F32),
                V((X, Y, Z), F32),
                V((X, Y, Z), F32),
                V((X * Y, 2 * Z), BF16),
                V((8, Z), F32),
                V((dims[0], Z), F32),
                V((dims[1] * dims[2], dims[0], Z), F32),
                V((NB * CAP, 2 * Z), F32),
                V((NB, CAP, Z), F32),
                V((NB, CAP, Z), F32),
                V((NB, CAP, Z), F32),
                V((NB, CAP, Z), F32),
                V((NB * CAP, X * Y), BF16),
                V((X * Y, NB * CAP), BF16),
                V((HR, NB * CAP), BF16),
                V((HR, Z), F32),
                dma((5,)), dma((2,)), dma((3, 5)), dma((3, 5)),
                dma, dma, dma, dma, dma, dma, dma, dma, dma((4,)),
            ],
            compiler_params=pltpu.CompilerParams(collective_id=0, has_side_effects=True, vmem_limit_bytes=60 * 1024 * 1024),
            name="hull_leapfrog",
        )(
            pressure, pressure_prev, buoyancy, kappa, hull_accel,
            row_block.reshape(1, HR), row_column.reshape(1, HR),
        )

    return jax.shard_map(
        local,
        mesh=mesh,
        in_specs=(
            P("gx", "gy", "blk"),
            P("gx", "gy", "blk"),
            P("gx", "gy", "blk"),
            P("gx", "gy", "blk"),
            P(("gx", "gy", "blk"), None),
            P(("gx", "gy", "blk"), None),
            P(("gx", "gy", "blk"), None),
        ),
        out_specs=(P("gx", "gy", "blk"), P(("gx", "gy", "blk"), None)),
        check_vma=False,
    )
```

time: 64.5 us -> 59.2 us (0.918)
  Pallas kernels: 61 us -> 55.8 us
    pallas_call x1, Pallas kernels: 61 us -> 55.8 us  [local(): pl.pallas_call(functools.partial(kernel, dims), out_shape=(jax.ShapeDtype...]
where the time goes in v1:
time: 59.2 us; the launch traced here: 59 us
  Pallas kernels  55.8 us (94%)
  local copies, waits for them, and re-layouts  2.63 us (4%)
  between operations  0.65 us (1%)
    pallas_call x1, Pallas kernels, local(): pl.pallas_call(functools.partial(kernel, dims), out_shape=(jax.ShapeDtype...  55.8 us
    unnamed x4, local copies, waits for them, and re-layouts  2.63 us

profile of v1, /device:TPU:1, one launch (start us, length us, event | category | flops | bytes accessed | tf_op | source)
XLA Modules:
  0.0 59.0 jit_solution(16928613928133895284)
XLA Ops:
  0.6 55.8 %hull_leapfrog.1 = (f32[16,64,128]{2,1,0:T(8,128)}, f32[512,128]{1,0:T(8,128)}) custom-call(f32[16,64,128]{2,1,0:T(8,128)} %p_hbm.1, f32[16,64,128]{2,1,0:T(8,128)} %prev_hbm.1, f32[16,64,128]{2,1,0:T(8,128)} %b_hbm.1, f32[16,64,128]{2,1,0:T(8,128)} %kap_hbm.1, f32[512,128]{1,0:T(8,128)} %hull_hbm.1, s32[1,512]{1,0:T(1,128)} %bitcast.2, s32[1,512]{1,0:T(1,128)} %bitcast.3), custom_call_target="tpu_custom_call" | custom-call | tf_op jit(solution)/shard_map/hull_leapfrog/pallas_call | solution.py:460
  56.4 0.0 copy-start
  56.4 1.9 %copy.11 = f32[16,64,128]{2,1,0:T(8,128)} copy(f32[16,64,128]{2,1,0:T(8,128)} %get-tuple-element.4) | data formatting | bytes 1048576
  58.3 0.0 copy-done
  58.3 0.7 %copy.12 = f32[512,128]{1,0:T(8,128)} copy(f32[512,128]{1,0:T(8,128)S(1)} %copy-done) | data formatting | bytes 524288
Async XLA Ops:
  56.4 1.9 %copy-start = (f32[512,128]{1,0:T(8,128)S(1)}, f32[512,128]{1,0:T(8,128)}, u32[]{:S(2)}) copy-start(f32[512,128]{1,0:T(8,128)} %get-tuple-element.5) | copy-start | bytes 786436

commit v2 on v1

--- a/solution.py
+++ b/solution.py
@@ -59,11 +59,11 @@
 
 def kernel(
     dims,
-    p_hbm, prev_hbm, b_hbm, kap_hbm, hull_hbm, rb_ref, rc_ref,
-    out_hbm, hp_hbm,
+    p_hbm, prev_hbm, b_hbm, kap_hbm, hull_hbm, rb_hbm, rc_hbm,
+    out_ref, hp_ref,
     E, EB, E2, ZS, ZR, PREV, KAP, HULL, FX, FY, TOT, BX, BY, BZ, BZO, NEXT,
-    CS, CR, CA, MC, SB, RV, PK, RET, Q, QT, PM, HOUT,
-    in_sem, out_sem, hs_sem, hr_sem, cs_sem, cr_sem, fs_sem, fr_sem, as_sem, ar_sem, bs_sem, br_sem, self_sem,
+    CS, CR, CA, MC, SB, RV, ROWS, PK, RET, Q, QT, PM, RB, RC,
+    in_sem, hs_sem, hr_sem, cs_sem, cr_sem, fs_sem, fr_sem, as_sem, ar_sem, bs_sem, br_sem, self_sem,
 ):
     nz, nx, ny = dims
     NB = nz * nx * ny
@@ -89,23 +89,31 @@
     zb = [(zi + nz - dz) % nz for dz in range(nz)]
     xb = [(xi + nx - dx) % nx for dx in range(nx)]
     yb = [(gy + ny - dy) % ny for dy in range(ny)]
-    half = nz // 2
-    order = [half]
-    for step in range(half - 1, 0, -1):
-        order += [step, nz - step]
-    order += [0]
     plane = [(dx, dy) for dx in range(nx) for dy in range(ny)]
 
+    def hops(offset):
+        return sum(min(d, n - d) for d, n in zip(offset, dims))
+
+    slots = sorted(
+        [(dz, dx, dy) for dz in range(nz) for dx, dy in plane],
+        key=lambda o: (-hops(o), o[0] % 2),
+    )
+    parts_n = 4
+    share = NB // parts_n
+
+    def group_of(k):
+        return k // share
+
     barrier = pltpu.get_barrier_semaphore()
-    for dz in order:
-        for dx, dy in plane:
-            if (dz, dx, dy) != (0, 0, 0):
-                pl.semaphore_signal(
-                    barrier, inc=1, device_id=(zs[dz] * nx + xs[dx], ys[dy], blk), device_id_type=MESH
-                )
+    for dz, dx, dy in slots[:-1]:
+        pl.semaphore_signal(
+            barrier, inc=1, device_id=(zs[dz] * nx + xs[dx], ys[dy], blk), device_id_type=MESH
+        )
     pl.semaphore_signal(barrier, inc=1, device_id=(gx, gy, 1 - blk), device_id_type=MESH)
 
     loads = [
+        pltpu.make_async_copy(rb_hbm, RB, in_sem.at[5]),
+        pltpu.make_async_copy(rc_hbm, RC, in_sem.at[6]),
         pltpu.make_async_copy(hull_hbm, HULL, in_sem.at[0]),
         pltpu.make_async_copy(p_hbm, E.at[pl.ds(3, X), pl.ds(8, Y)], in_sem.at[1]),
         pltpu.make_async_copy(b_hbm, EB.at[pl.ds(2, X), pl.ds(8, Y)], in_sem.at[2]),
@@ -132,7 +140,9 @@
         def _(ref=ref, w=w):
             ref[w : w + X, 8 + Y :] = jnp.zeros((X, 8, LANES), F32)
 
-    rb = rb_ref[...]
+    loads[0].wait()
+    loads[1].wait()
+    rb = RB[...]
     owner = onehot(jnp.broadcast_to(rb, (NB, HR)) == lax.broadcasted_iota(jnp.int32, (NB, HR), 0))
     before = onehot(
         lax.broadcasted_iota(jnp.int32, (HR, HR), 0) < lax.broadcasted_iota(jnp.int32, (HR, HR), 1)
@@ -140,7 +150,7 @@
     earlier = dot(owner, before)
     slot = jnp.sum(owner.astype(F32) * earlier, axis=0, keepdims=True).astype(jnp.int32)
     placing = rb * CAP + slot
-    code = rc_ref[...] + 1
+    code = RC[...] + 1
     row_z = lax.broadcasted_iota(jnp.int32, (16, HR), 0)
     which_z = jnp.broadcast_to(placing // GS, (16, HR))
     coded = jnp.where(row_z == which_z, jnp.broadcast_to(code // 32, (16, HR)), 0) + jnp.where(
@@ -150,7 +160,7 @@
     sums = dot_nt(coded.astype(F32).astype(BF16), lane_of)
     CS[...] = sums[0:8] * 32.0 + sums[8:16]
 
-    loads[0].wait()
+    loads[2].wait()
     hull_parts = parts(HULL[...])
 
     def pack(m, _):
@@ -174,8 +184,8 @@
                     acc = jnp.where(edge == m, pltpu.roll(tile, 4 * m, 1) if m else tile, acc)
             ZS[field, q] = acc
 
-    loads[1].wait()
-    loads[2].wait()
+    loads[3].wait()
+    loads[4].wait()
     gather_edge(0, E, 3)
     gather_edge(1, EB, 2)
 
@@ -192,10 +202,10 @@
                 ref.at[pl.ds(lo, width), pl.ds(8, Y)], ref.at[pl.ds(X + lo, width), pl.ds(8, Y)],
                 send.at[1], recv.at[1], device_id=(jnp.maximum(gx - 1, 0), gy, blk), device_id_type=MESH)),
             (gy < ny - 1, gy > 0, pltpu.make_async_remote_copy(
-                ref.at[pl.ds(lo, X), pl.ds(Y, 8)], ref.at[pl.ds(lo, X), pl.ds(0, 8)],
+                ref.at[pl.ds(lo, X), pl.ds(Y + 8 - width, width)], ref.at[pl.ds(lo, X), pl.ds(8 - width, width)],
                 send.at[2], recv.at[2], device_id=(gx, jnp.minimum(gy + 1, ny - 1), blk), device_id_type=MESH)),
             (gy > 0, gy < ny - 1, pltpu.make_async_remote_copy(
-                ref.at[pl.ds(lo, X), pl.ds(8, 8)], ref.at[pl.ds(lo, X), pl.ds(8 + Y, 8)],
+                ref.at[pl.ds(lo, X), pl.ds(8, width)], ref.at[pl.ds(lo, X), pl.ds(8 + Y, width)],
                 send.at[3], recv.at[3], device_id=(gx, jnp.maximum(gy - 1, 0), blk), device_id_type=MESH)),
             (None, None, pltpu.make_async_remote_copy(
                 ZS.at[field], ZR.at[field],
@@ -234,17 +244,13 @@
     start(halo_p)
     start(halo_b)
 
-    for dz in order:
-        for dx, dy in plane:
-            k = (dz * nx + dx) * ny + dy
-            if k == 0:
-                continue
-            dest_gx = zs[dz] * nx + xs[dx]
-            pltpu.make_async_remote_copy(
-                SB.at[dest_gx * ny + ys[dy]], RV.at[k], as_sem, ar_sem,
-                device_id=(dest_gx, ys[dy], blk), device_id_type=MESH,
-            ).start()
-    own = pltpu.make_async_copy(SB.at[me], RV.at[0], self_sem.at[1])
+    for k, (dz, dx, dy) in enumerate(slots[:-1]):
+        dest_gx = zs[dz] * nx + xs[dx]
+        pltpu.make_async_remote_copy(
+            SB.at[dest_gx * ny + ys[dy]], RV.at[k], as_sem, ar_sem.at[group_of(k)],
+            device_id=(dest_gx, ys[dy], blk), device_id_type=MESH,
+        ).start()
+    own = pltpu.make_async_copy(SB.at[me], RV.at[NB - 1], self_sem.at[1])
     own.start()
 
     drained(CR.at[pl.ds(0, nz - 1)], cr_sem)
@@ -257,18 +263,28 @@
     own_tile = pltpu.make_async_copy(CR, CA.at[0], self_sem.at[2])
     own_tile.start()
 
+    rel_z = (placing // GS + (nz - zi)) % nz
+    rel_x = (placing // (CAP * ny) % nx + (nx - xi)) % nx
+    rel_y = (placing // CAP % ny + (ny - gy)) % ny
+    relative = ((rel_z * nx + rel_x) * ny + rel_y) * CAP + placing % CAP
     weights_row = lax.broadcasted_iota(jnp.int32, (16, LANES), 0)
     place_row = lax.broadcasted_iota(jnp.int32, (16, HR), 0)
     place_code = jnp.where(
-        place_row == 0, jnp.broadcast_to(placing // 32, (16, HR)),
-        jnp.where(place_row == 1, jnp.broadcast_to(placing % 32, (16, HR)), 0),
+        place_row == 0, jnp.broadcast_to(relative // 32, (16, HR)),
+        jnp.where(place_row == 1, jnp.broadcast_to(relative % 32, (16, HR)), 0),
     ).astype(F32).astype(BF16)
     place_w = jnp.where(weights_row == 0, 32.0, jnp.where(weights_row == 1, 1.0, 0.0)).astype(BF16)
     placing_col = dot_tn(place_code, place_w)
     span = min(LANES, NB * CAP)
     for m in range(NB * CAP // span):
-        cell = (lax.broadcasted_iota(jnp.int32, (HR, span), 1) + m * span).astype(F32)
-        PM[:, m * span : (m + 1) * span] = onehot(placing_col[:, :span] == cell)
+        spot_lane = lax.broadcasted_iota(jnp.int32, (8, span), 1)
+        label = spot_lane % CAP
+        for j in range(span // CAP):
+            dz, dx, dy = slots[m * (span // CAP) + j]
+            base = ((dz * nx + dx) * ny + dy) * CAP
+            label = jnp.where(spot_lane // CAP == j, label + base, label)
+        label = jnp.broadcast_to(label[0:1], (HR, span)).astype(F32)
+        PM[:, m * span : (m + 1) * span] = onehot(placing_col[:, :span] == label)
 
     lane = lax.broadcasted_iota(jnp.int32, (Y, LANES), 1)
     halo_lanes = (lane < LANES // 2) == (jnp.broadcast_to(blk, (Y, LANES)) == 0)
@@ -315,36 +331,37 @@
         for c in (0, 1, 2, X, X + 1, X + 2):
             flux_x(src, c)
 
-    def across(src, field):
+    def across_z(src, field):
         def body(q, _):
             for i in range(PER):
                 c = q * PER + i
-                FY[i] = wide(src[c + 3, 5 : 13 + Y], src[c + 3, 6 : 14 + Y], src[c + 3, 7 : 15 + Y], src[c + 3, 8 : 16 + Y]) * BY[c]
                 near = src[c + 3, 8 : 8 + Y]
                 far = beside(field, q, i)
                 flux = wide(down(1, near, far), near, up(1, near, far), up(2, near, far)) * BZ[c]
                 beyond = wide(down(1, far, near), far, up(1, far, near), up(2, far, near)) * BZO[c]
-                TOT[c] = wide(FY[i, 0:Y], FY[i, 1 : 1 + Y], FY[i, 2 : 2 + Y], FY[i, 3 : 3 + Y]) + wide(
-                    down(2, flux, beyond), down(1, flux, beyond), flux, up(1, flux, beyond)
-                )
+                TOT[c] = wide(down(2, flux, beyond), down(1, flux, beyond), flux, up(1, flux, beyond))
             return 0
 
         lax.fori_loop(0, X // PER, body, 0)
+
+    def across_y(src, c, i):
+        FY[i] = wide(src[c + 3, 5 : 13 + Y], src[c + 3, 6 : 14 + Y], src[c + 3, 7 : 15 + Y], src[c + 3, 8 : 16 + Y]) * BY[c]
+        return wide(FY[i, 0:Y], FY[i, 1 : 1 + Y], FY[i, 2 : 2 + Y], FY[i, 3 : 3 + Y])
 
     def laplace(c):
         return TOT[c] + wide(FX[c], FX[c + 1], FX[c + 2], FX[c + 3])
 
-    loads[3].wait()
-    loads[4].wait()
+    loads[5].wait()
+    loads[6].wait()
     finish(halo_p)
     inner_x(E)
     outer_x(E)
-    across(E, 0)
+    across_z(E, 0)
 
     def first(q, _):
         for i in range(PER):
             c = q * PER + i
-            E2[c + 3, 8 : 8 + Y] = 2.0 * E[c + 3, 8 : 8 + Y] - PREV[c] + KAP[c] * laplace(c)
+            E2[c + 3, 8 : 8 + Y] = 2.0 * E[c + 3, 8 : 8 + Y] - PREV[c] + KAP[c] * (laplace(c) + across_y(E, c, i))
         return 0
 
     lax.fori_loop(0, X // PER, first, 0)
@@ -352,13 +369,11 @@
     drained(CA.at[pl.ds(0, G - 1)], fr_sem)
     own_tile.wait()
     keep = lane8 == lax.broadcasted_iota(jnp.int32, (8, LANES), 0) + spot * CAP
-    for dz in range(nz):
-        for j in range(G):
-            line = jnp.where(keep, jnp.broadcast_to(CA[j, dz : dz + 1, :], (8, LANES)), 0.0)
-            high = jnp.floor(line * (1.0 / 32.0))
-            at = (dz * G + j) * 8
-            MC[at : at + 8, 0:LANES] = high
-            MC[at : at + 8, LANES:] = line - 32.0 * high
+    for k, (dz, dx, dy) in enumerate(slots):
+        line = jnp.where(keep, jnp.broadcast_to(CA[dx * ny + dy, dz : dz + 1, :], (8, LANES)), 0.0)
+        high = jnp.floor(line * (1.0 / 32.0))
+        MC[k * 8 : k * 8 + 8, 0:LANES] = high
+        MC[k * 8 : k * 8 + 8, LANES:] = line - 32.0 * high
     w_lane = jnp.where(lax.broadcasted_iota(jnp.int32, (8, 2 * LANES), 1) < LANES, 32.0, 1.0).astype(BF16)
     w_full = jnp.where(lax.broadcasted_iota(jnp.int32, (2 * LANES, LANES), 0) < LANES, 32.0, 1.0).astype(BF16)
     col_lane = dot_nt(w_lane, MC[...].astype(BF16))[0:1].astype(jnp.int32) - 1
@@ -380,69 +395,117 @@
 
     lax.fori_loop(0, nz, build_q, 0)
 
-    drained(RV.at[pl.ds(0, NB - 1)], ar_sem)
-    own.wait()
-    rows = parts(RV[...].reshape(NB * CAP, LANES))
+    for n in range(parts_n):
+        last = n == parts_n - 1
+        drained(RV.at[pl.ds(0, share - 1 if last else share)], ar_sem.at[n])
+        if last:
+            own.wait()
+        ROWS[n * share * CAP : (n + 1) * share * CAP] = parts(
+            RV[n * share : (n + 1) * share].reshape(share * CAP, LANES)
+        )
     halo_m = shares(E2, 2, 3)
 
-    def middle(q, _):
-        pushed = joined(dot(QT[pl.ds(q * PER * Y, PER * Y)], rows)).reshape(PER, Y, LANES)
+    def middle(q):
+        pushed = joined(dot(QT[q * PER * Y : (q + 1) * PER * Y], ROWS[...])).reshape(PER, Y, LANES)
         for i in range(PER):
             c = q * PER + i
             force = (GAIN * KAP[c]) * pushed[i]
             E2[c + 3, 8 : 8 + Y] = E2[c + 3, 8 : 8 + Y] + force
             PREV[c] = force - E[c + 3, 8 : 8 + Y]
-        return 0
-
-    lax.fori_loop(0, X // PER, middle, 0)
-    start(halo_m[0:4])
+
+    quads = X // PER
+    ends = sorted({0, quads - 1})
+    inside = [q for q in range(quads) if q not in ends]
+    for q in ends:
+        middle(q)
+    start(halo_m[0:2])
+    for q in inside:
+        middle(q)
+    start(halo_m[2:4])
     gather_edge(2, E2, 3)
     start(halo_m[4:5])
     inner_x(E2)
     finish(halo_m[4:5])
+    across_z(E2, 2)
     finish(halo_m[2:4])
-    across(E2, 2)
+
+    def second(q, with_y):
+        for i in range(PER):
+            c = q * PER + i
+            total = laplace(c)
+            if with_y:
+                total = total + across_y(E2, c, i)
+            val = 2.0 * E2[c + 3, 8 : 8 + Y] + PREV[c] + KAP[c] * total
+            out_ref[c] = val
+            hi, lo = split2(val)
+            NEXT[c * Y : (c + 1) * Y, 0:LANES] = hi
+            NEXT[c * Y : (c + 1) * Y, LANES : 2 * LANES] = lo
+
+    for q in inside:
+        second(q, True)
+    for q in ends:
+        for i in range(PER):
+            c = q * PER + i
+            TOT[c] = TOT[c] + across_y(E2, c, i)
+
+    pieces = max(parts_n, NB * CAP // LANES)
+    count = NB // pieces
+
+    def pick(n, quad):
+        at = slice(quad * PER * Y, (quad + 1) * PER * Y)
+        return joined(dot(Q[n * count * CAP : (n + 1) * count * CAP, at], NEXT[at])).reshape(count, 8, LANES)
+
+    for n in range(pieces):
+        total = None
+        for q in inside:
+            total = pick(n, q) if total is None else total + pick(n, q)
+        if total is not None:
+            PK[n * count : (n + 1) * count] = total
     finish(halo_m[0:2])
     outer_x(E2)
-
-    def second(q, _):
-        for i in range(PER):
-            c = q * PER + i
-            val = 2.0 * E2[c + 3, 8 : 8 + Y] + PREV[c] + KAP[c] * laplace(c)
-            TOT[c] = val
-            hi, lo = split2(val)
-            NEXT[pl.ds(c * Y, Y), 0:LANES] = hi
-            NEXT[pl.ds(c * Y, Y), LANES : 2 * LANES] = lo
-        return 0
-
-    lax.fori_loop(0, X // PER, second, 0)
-    out_copy = pltpu.make_async_copy(TOT, out_hbm, out_sem.at[0])
-    out_copy.start()
-
-    for dz in order:
-        PK[dz * G : (dz + 1) * G] = joined(dot(Q[dz * GS : (dz + 1) * GS], NEXT[...])).reshape(G, 8, LANES)
-        for dx, dy in plane:
-            k = (dz * nx + dx) * ny + dy
-            if k == 0:
-                continue
-            pltpu.make_async_remote_copy(
-                PK.at[k], RET.at[me], bs_sem, br_sem,
-                device_id=(zb[dz] * nx + xb[dx], yb[dy], blk), device_id_type=MESH,
-            ).start()
-    back = pltpu.make_async_copy(PK.at[0], RET.at[me], self_sem.at[3])
+    for q in ends:
+        second(q, False)
+
+    for n in range(pieces):
+        total = None
+        for q in ends:
+            total = pick(n, q) if total is None else total + pick(n, q)
+        if inside:
+            total = total + PK[n * count : (n + 1) * count]
+        PK[n * count : (n + 1) * count] = total
+        for k in range(n * count, (n + 1) * count):
+            dz, dx, dy = slots[k]
+            if k < NB - 1:
+                pltpu.make_async_remote_copy(
+                    PK.at[k], RET.at[k], bs_sem, br_sem.at[group_of(k)],
+                    device_id=(zb[dz] * nx + xb[dx], yb[dy], blk), device_id_type=MESH,
+                ).start()
+    back = pltpu.make_async_copy(PK.at[NB - 1], RET.at[NB - 1], self_sem.at[3])
     back.start()
 
     drained(CR.at[pl.ds(0, nz - 1)], cs_sem)
     drained(CA.at[pl.ds(0, G - 1)], fs_sem)
     drained(SB.at[pl.ds(0, NB - 1)], as_sem)
+    for n in range(parts_n):
+        last = n == parts_n - 1
+        drained(RET.at[pl.ds(0, share - 1 if last else share)], br_sem.at[n])
+        if last:
+            back.wait()
+        at = slice(n * share * CAP, (n + 1) * share * CAP)
+        got = joined(dot(PM[:, at], parts(RET[n * share : (n + 1) * share].reshape(share * CAP, LANES))))
+        hp_ref[...] = got if n == 0 else hp_ref[...] + got
     drained(PK.at[pl.ds(0, NB - 1)], bs_sem)
-    drained(RET.at[pl.ds(0, NB - 1)], br_sem)
-    back.wait()
-    HOUT[...] = joined(dot(PM[...], parts(RET[...].reshape(NB * CAP, LANES))))
-    hull_copy = pltpu.make_async_copy(HOUT, hp_hbm, out_sem.at[1])
-    hull_copy.start()
-    hull_copy.wait()
-    out_copy.wait()
+
+
+def keep_out(field, rows, field_out, rows_out, sem):
+    copies = [
+        pltpu.make_async_copy(field, field_out, sem.at[0]),
+        pltpu.make_async_copy(rows, rows_out, sem.at[1]),
+    ]
+    for copy in copies:
+        copy.start()
+    for copy in copies:
+        copy.wait()
 
 
 def solution(mesh):
@@ -453,18 +516,18 @@
     def local(pressure, pressure_prev, buoyancy, kappa, hull_accel, row_block, row_column):
         X, Y, Z = pressure.shape
         HR = hull_accel.shape[0]
-        any_spec = pl.BlockSpec(memory_space=pl.ANY)
+        any_spec = pl.BlockSpec(memory_space=pltpu.HBM)
         vmem_spec = pl.BlockSpec(memory_space=pltpu.VMEM)
         dma = pltpu.SemaphoreType.DMA
         V = pltpu.VMEM
-        return pl.pallas_call(
+        results = pl.pallas_call(
             functools.partial(kernel, dims),
             out_shape=(
                 jax.ShapeDtypeStruct((X, Y, Z), F32),
                 jax.ShapeDtypeStruct((HR, Z), F32),
             ),
-            in_specs=[any_spec] * 5 + [vmem_spec] * 2,
-            out_specs=[any_spec] * 2,
+            in_specs=[any_spec] * 7,
+            out_specs=[vmem_spec] * 2,
             scratch_shapes=[
                 V((X + 6, Y + 16, Z), F32),
                 V((X + 4, Y + 16, Z), F32),
@@ -488,21 +551,37 @@
                 V((NB * CAP, 2 * Z), F32),
                 V((NB, CAP, Z), F32),
                 V((NB, CAP, Z), F32),
+                V((NB * CAP, 2 * Z), BF16),
                 V((NB, CAP, Z), F32),
                 V((NB, CAP, Z), F32),
                 V((NB * CAP, X * Y), BF16),
                 V((X * Y, NB * CAP), BF16),
                 V((HR, NB * CAP), BF16),
-                V((HR, Z), F32),
-                dma((5,)), dma((2,)), dma((3, 5)), dma((3, 5)),
-                dma, dma, dma, dma, dma, dma, dma, dma, dma((4,)),
+                V((1, HR), jnp.int32),
+                V((1, HR), jnp.int32),
+                dma((7,)), dma((3, 5)), dma((3, 5)),
+                dma, dma, dma, dma, dma, dma((4,)), dma, dma((4,)), dma((4,)),
             ],
-            compiler_params=pltpu.CompilerParams(collective_id=0, has_side_effects=True, vmem_limit_bytes=60 * 1024 * 1024),
+            compiler_params=pltpu.CompilerParams(collective_id=0, has_side_effects=True, vmem_limit_bytes=36 * 1024 * 1024),
             name="hull_leapfrog",
         )(
-            pressure, pressure_prev, buoyancy, kappa, hull_accel,
-            row_block.reshape(1, HR), row_column.reshape(1, HR),
+            *(pltpu.with_memory_space_constraint(v, pltpu.HBM) for v in (
+                pressure, pressure_prev, buoyancy, kappa, hull_accel,
+                row_block.reshape(1, HR), row_column.reshape(1, HR),
+            ))
         )
+        return pl.pallas_call(
+            keep_out,
+            out_shape=(
+                jax.ShapeDtypeStruct((X, Y, Z), F32),
+                jax.ShapeDtypeStruct((HR, Z), F32),
+            ),
+            in_specs=[vmem_spec] * 2,
+            out_specs=[any_spec] * 2,
+            scratch_shapes=[dma((2,))],
+            compiler_params=pltpu.CompilerParams(vmem_limit_bytes=2 * 1024 * 1024),
+            name="write_out",
+        )(*results)
 
     return jax.shard_map(
         local,

time: 59.2 us -> 55.5 us (0.938)
  local copies, waits for them, and re-layouts: 2.63 us -> 0 us
  Pallas kernels: 55.8 us -> 54.8 us
    unnamed x4 -> x0, local copies, waits for them, and re-layouts: 2.63 us -> none
    pallas_call x1, Pallas kernels: 55.8 us -> 53.9 us  [local(): pl.pallas_call(functools.partial(kernel, dims), out_shape=(jax.ShapeDtype...]
    pallas_call x0 -> x1, Pallas kernels: none -> 0.89 us  [local(): pl.pallas_call(keep_out, out_shape=(jax.ShapeDtypeStruct((X, Y, Z), F32),...]
where the time goes in v2:
time: 55.5 us; the launch traced here: 55.4 us
  Pallas kernels  54.8 us (99%)
  between operations  0.64 us (1%)
    pallas_call x1, Pallas kernels, local(): pl.pallas_call(functools.partial(kernel, dims), out_shape=(jax.ShapeDtype...  53.9 us

profile of v2, /device:TPU:1, one launch (start us, length us, event | category | flops | bytes accessed | tf_op | source)
XLA Modules:
  0.0 55.4 jit_solution(9692144114322707203)
XLA Ops:
  0.6 53.9 %hull_leapfrog.1 = (f32[16,64,128]{2,1,0:T(8,128)S(1)}, f32[512,128]{1,0:T(8,128)S(1)}) custom-call(f32[16,64,128]{2,1,0:T(8,128)} %p_hbm.1, f32[16,64,128]{2,1,0:T(8,128)} %prev_hbm.1, f32[16,64,128]{2,1,0:T(8,128)} %b_hbm.1, f32[16,64,128]{2,1,0:T(8,128)} %kap_hbm.1, f32[512,128]{1,0:T(8,128)} %hull_hbm.1, s32[1,512]{1,0:T(1,128)} %bitcast.2, s32[1,512]{1,0:T(1,128)} %bitcast.3), custom_call_target="tpu_custom_call" | custom-call | tf_op jit(solution)/shard_map/hull_leapfrog/pallas_call | solution.py:523
  54.5 0.9 %write_out.1 = (f32[16,64,128]{2,1,0:T(8,128)}, f32[512,128]{1,0:T(8,128)}) custom-call(f32[16,64,128]{2,1,0:T(8,128)S(1)} %get-tuple-element.4.field, f32[512,128]{1,0:T(8,128)S(1)} %get-tuple-element.5.rows), custom_call_target="tpu_custom_call" | custom-call | tf_op jit(solution)/shard_map/write_out/pallas_call | solution.py:573

commit v3 on v2

--- a/solution.py
+++ b/solution.py
@@ -61,7 +61,7 @@
     dims,
     p_hbm, prev_hbm, b_hbm, kap_hbm, hull_hbm, rb_hbm, rc_hbm,
     out_ref, hp_ref,
-    E, EB, E2, ZS, ZR, PREV, KAP, HULL, FX, FY, TOT, BX, BY, BZ, BZO, NEXT,
+    E, EB, E2, ZS, ZR, SPLIT, ZW, ZB, PREV, KAP, HULL, FX, FY, TOT, BX, BY, BZ, NEXT,
     CS, CR, CA, MC, SB, RV, ROWS, PK, RET, Q, QT, PM, RB, RC,
     in_sem, hs_sem, hr_sem, cs_sem, cr_sem, fs_sem, fr_sem, as_sem, ar_sem, bs_sem, br_sem, self_sem,
 ):
@@ -104,13 +104,6 @@
     def group_of(k):
         return k // share
 
-    barrier = pltpu.get_barrier_semaphore()
-    for dz, dx, dy in slots[:-1]:
-        pl.semaphore_signal(
-            barrier, inc=1, device_id=(zs[dz] * nx + xs[dx], ys[dy], blk), device_id_type=MESH
-        )
-    pl.semaphore_signal(barrier, inc=1, device_id=(gx, gy, 1 - blk), device_id_type=MESH)
-
     loads = [
         pltpu.make_async_copy(rb_hbm, RB, in_sem.at[5]),
         pltpu.make_async_copy(rc_hbm, RC, in_sem.at[6]),
@@ -122,6 +115,13 @@
     ]
     for load in loads:
         load.start()
+
+    barrier = pltpu.get_barrier_semaphore()
+    for dz, dx, dy in slots[:-1]:
+        pl.semaphore_signal(
+            barrier, inc=1, device_id=(zs[dz] * nx + xs[dx], ys[dy], blk), device_id_type=MESH
+        )
+    pl.semaphore_signal(barrier, inc=1, device_id=(gx, gy, 1 - blk), device_id_type=MESH)
 
     for ref, w in ((E, 3), (EB, 2), (E2, 3)):
         @pl.when(gx == 0)
@@ -171,23 +171,33 @@
 
     lax.fori_loop(0, nz, pack, 0)
 
-    lane8 = lax.broadcasted_iota(jnp.int32, (8, LANES), 1)
-    edge = jnp.where(jnp.broadcast_to(blk, (8, LANES)) == 0, (lane8 + 3) % LANES, lane8) // 4
-
-    def gather_edge(field, ref, lo):
-        for q in range(X // PER):
-            acc = jnp.zeros((8, LANES), F32)
-            for i in range(PER):
-                for t in range(T):
-                    m = i * T + t
-                    tile = ref[lo + q * PER + i, 8 + 8 * t : 16 + 8 * t]
-                    acc = jnp.where(edge == m, pltpu.roll(tile, 4 * m, 1) if m else tile, acc)
-            ZS[field, q] = acc
+    e_row = lax.broadcasted_iota(jnp.int32, (8, 2 * LANES), 0)
+    e_lane = lax.broadcasted_iota(jnp.int32, (8, 2 * LANES), 1) % LANES
+    first_sent = jnp.broadcast_to((1 - blk) * (LANES - 3), (8, 2 * LANES))
+    wanted = jnp.where(e_row < 3, first_sent + e_row, jnp.where(e_row < 5, e_row - 3, e_row + (LANES - 7)))
+    edge_w = onehot((e_lane == wanted) & (e_row < 7))
+
+    def split_planes(ref, lo, q):
+        at = pl.ds(q * PER * Y, PER * Y)
+        planes = [ref[q * PER + i + lo, 8 : 8 + Y] for i in range(PER)]
+        SPLIT[at] = parts(jnp.concatenate(planes, axis=0))
+
+    def gather_edge(field):
+        ZS[field] = dot_nt(edge_w, SPLIT[...])
+
+    def all_planes(ref, lo):
+        def body(q, _):
+            split_planes(ref, lo, q)
+            return 0
+
+        lax.fori_loop(0, X // PER, body, 0)
 
     loads[3].wait()
     loads[4].wait()
-    gather_edge(0, E, 3)
-    gather_edge(1, EB, 2)
+    all_planes(EB, 2)
+    gather_edge(1)
+    all_planes(E, 3)
+    gather_edge(0)
 
     pl.semaphore_wait(barrier, NB)
 
@@ -286,24 +296,83 @@
         label = jnp.broadcast_to(label[0:1], (HR, span)).astype(F32)
         PM[:, m * span : (m + 1) * span] = onehot(placing_col[:, :span] == label)
 
-    lane = lax.broadcasted_iota(jnp.int32, (Y, LANES), 1)
-    halo_lanes = (lane < LANES // 2) == (jnp.broadcast_to(blk, (Y, LANES)) == 0)
-
-    def beside(field, q, i):
-        packed = ZR[field, q]
-        tiles = []
-        for t in range(T):
-            m = i * T + t
-            tiles.append(pltpu.roll(packed, LANES - 4 * m, 1) if m else packed)
-        return jnp.where(halo_lanes, jnp.concatenate(tiles, axis=0), 0.0)
-
-    def up(k, near, far):
-        return pltpu.roll(jnp.where(lane < k, far, near), LANES - k, 1)
-
-    def down(k, near, far):
-        return pltpu.roll(jnp.where(lane >= LANES - k, far, near), k, 1)
+    w_row = lax.broadcasted_iota(jnp.int32, (2 * LANES, LANES), 0) % LANES
+    w_col = lax.broadcasted_iota(jnp.int32, (2 * LANES, LANES), 1)
+
+    def band(shift):
+        at = w_row - w_col - shift
+        val = jnp.where(at == 0, 27.0, jnp.where(at == -1, -27.0, 0.0))
+        return (val + jnp.where(at == 1, -1.0, jnp.where(at == -2, 1.0, 0.0))).astype(BF16)
+
+    ZW[0] = band(1)
+    ZW[1] = band(0)
+    f_row = lax.broadcasted_iota(jnp.int32, (16, LANES), 0) % 8
+    f_lane = lax.broadcasted_iota(jnp.int32, (16, LANES), 1)
+    fix_lane = jnp.where(f_row < 3, f_row, (LANES + 2) - f_row)
+    fix_w = onehot((f_lane == fix_lane) & (f_row < 6))
+    left_on = blk.astype(F32)
+    right_on = 1.0 - left_on
+
+    def along_z(q):
+        at = pl.ds(q * PER * Y, PER * Y)
+        slope = dot(SPLIT[at], ZW[0])
+        flux = slope * jnp.concatenate([BZ[q * PER + i] for i in range(PER)], axis=0)
+        val = dot(parts(flux), ZW[1]).reshape(PER, Y, LANES)
+        for i in range(PER):
+            TOT[q * PER + i] = val[i]
+
+    def fix_z(field):
+        def halo(r):
+            return ZR[field, r : r + 1]
+
+        def own(r):
+            return ZS[field, r : r + 1]
+
+        a3, a2, a1 = (halo(r) * left_on for r in range(3))
+        n0, n1, n2 = (halo(r) * right_on for r in range(3))
+        v0, v1, v_prev, v_last = own(3), own(4), own(5), own(6)
+        at0 = ZB[0:1] * a1
+        before1 = ZB[1:2] * (27.0 * (v0 - a1) - (v1 - a2))
+        before2 = ZB[2:3] * (27.0 * (a1 - a2) - (v0 - a3))
+        end1 = ZB[4:5] * (27.0 * (n0 - v_last) - (n1 - v_prev))
+        end2 = ZB[3:4] * n0
+        after = ZB[5:6] * (27.0 * (n1 - n0) - (n2 - v_last))
+        rows = [
+            27.0 * (at0 - before1) + before2,
+            before1 - 27.0 * at0,
+            at0,
+            27.0 * (end1 + end2) - after,
+            -27.0 * end2 - end1,
+            end2,
+            jnp.zeros_like(at0),
+            jnp.zeros_like(at0),
+        ]
+        hi, lo = split2(jnp.concatenate(rows, axis=0))
+        return jnp.concatenate([hi.astype(F32), lo.astype(F32)], axis=0).astype(BF16)
+
+    def add_fix(fixes, q):
+        val = dot_tn(fixes[:, q * PER * Y : (q + 1) * PER * Y], fix_w).reshape(PER, Y, LANES)
+        for i in range(PER):
+            TOT[q * PER + i] = TOT[q * PER + i] + val[i]
 
     finish(halo_b)
+
+    inner_lane = lax.broadcasted_iota(jnp.int32, (Y, LANES), 1) < LANES - 1
+    b_left = [ZR[1, r : r + 1] * left_on for r in (1, 2)]
+    b_right = [ZR[1, r : r + 1] * right_on for r in (0, 1)]
+    own_edge = [ZS[1, r : r + 1] for r in range(3, 7)]
+    ZB[...] = FACE * jnp.concatenate(
+        [
+            own_edge[0] + own_edge[1],
+            b_left[1] + own_edge[0],
+            b_left[0] + b_left[1],
+            own_edge[2] + own_edge[3],
+            own_edge[3] + b_right[0],
+            b_right[0] + b_right[1],
+            jnp.zeros((2, cells), F32),
+        ],
+        axis=0,
+    )
 
     def faces(q, _):
         for i in range(PER):
@@ -311,9 +380,7 @@
             BX[c] = (EB[c, 8 : 8 + Y] + EB[c + 1, 8 : 8 + Y]) * FACE
             BY[c] = (EB[c + 2, 6 : 14 + Y] + EB[c + 2, 7 : 15 + Y]) * FACE
             own_b = EB[c + 2, 8 : 8 + Y]
-            far_b = beside(1, q, i)
-            BZ[c] = (own_b + up(1, own_b, far_b)) * FACE
-            BZO[c] = (far_b + up(1, far_b, own_b)) * FACE
+            BZ[c] = jnp.where(inner_lane, own_b + pltpu.roll(own_b, LANES - 1, 1), 0.0) * FACE
         return 0
 
     lax.fori_loop(0, X // PER, faces, 0)
@@ -330,19 +397,6 @@
     def outer_x(src):
         for c in (0, 1, 2, X, X + 1, X + 2):
             flux_x(src, c)
-
-    def across_z(src, field):
-        def body(q, _):
-            for i in range(PER):
-                c = q * PER + i
-                near = src[c + 3, 8 : 8 + Y]
-                far = beside(field, q, i)
-                flux = wide(down(1, near, far), near, up(1, near, far), up(2, near, far)) * BZ[c]
-                beyond = wide(down(1, far, near), far, up(1, far, near), up(2, far, near)) * BZO[c]
-                TOT[c] = wide(down(2, flux, beyond), down(1, flux, beyond), flux, up(1, flux, beyond))
-            return 0
-
-        lax.fori_loop(0, X // PER, body, 0)
 
     def across_y(src, c, i):
         FY[i] = wide(src[c + 3, 5 : 13 + Y], src[c + 3, 6 : 14 + Y], src[c + 3, 7 : 15 + Y], src[c + 3, 8 : 16 + Y]) * BY[c]
@@ -356,7 +410,10 @@
     finish(halo_p)
     inner_x(E)
     outer_x(E)
-    across_z(E, 0)
+    fixes = fix_z(0)
+    for q in range(X // PER):
+        along_z(q)
+        add_fix(fixes, q)
 
     def first(q, _):
         for i in range(PER):
@@ -368,7 +425,7 @@
 
     drained(CA.at[pl.ds(0, G - 1)], fr_sem)
     own_tile.wait()
-    keep = lane8 == lax.broadcasted_iota(jnp.int32, (8, LANES), 0) + spot * CAP
+    keep = lax.broadcasted_iota(jnp.int32, (8, LANES), 1) == lax.broadcasted_iota(jnp.int32, (8, LANES), 0) + spot * CAP
     for k, (dz, dx, dy) in enumerate(slots):
         line = jnp.where(keep, jnp.broadcast_to(CA[dx * ny + dy, dz : dz + 1, :], (8, LANES)), 0.0)
         high = jnp.floor(line * (1.0 / 32.0))
@@ -410,7 +467,9 @@
         for i in range(PER):
             c = q * PER + i
             force = (GAIN * KAP[c]) * pushed[i]
-            E2[c + 3, 8 : 8 + Y] = E2[c + 3, 8 : 8 + Y] + force
+            mid = E2[c + 3, 8 : 8 + Y] + force
+            E2[c + 3, 8 : 8 + Y] = mid
+            SPLIT[c * Y : (c + 1) * Y] = parts(mid)
             PREV[c] = force - E[c + 3, 8 : 8 + Y]
 
     quads = X // PER
@@ -422,11 +481,15 @@
     for q in inside:
         middle(q)
     start(halo_m[2:4])
-    gather_edge(2, E2, 3)
+    gather_edge(2)
     start(halo_m[4:5])
     inner_x(E2)
+    for q in range(quads):
+        along_z(q)
     finish(halo_m[4:5])
-    across_z(E2, 2)
+    fixes = fix_z(2)
+    for q in range(quads):
+        add_fix(fixes, q)
     finish(halo_m[2:4])
 
     def second(q, with_y):
@@ -532,8 +595,11 @@
                 V((X + 6, Y + 16, Z), F32),
                 V((X + 4, Y + 16, Z), F32),
                 V((X + 6, Y + 16, Z), F32),
-                V((3, X * Y // 256, 8, Z), F32),
-                V((3, X * Y // 256, 8, Z), F32),
+                V((3, 8, X * Y), F32),
+                V((3, 8, X * Y), F32),
+                V((X * Y, 2 * Z), BF16),
+                V((2, 2 * Z, Z), BF16),
+                V((8, X * Y), F32),
                 V((X, Y, Z), F32),
                 V((X, Y, Z), F32),
                 V((HR, Z), F32),
@@ -542,7 +608,6 @@
                 V((X, Y, Z), F32),
                 V((X + 3, Y, Z), F32),
                 V((X, Y + 8, Z), F32),
-                V((X, Y, Z), F32),
                 V((X, Y, Z), F32),
                 V((X * Y, 2 * Z), BF16),
                 V((8, Z), F32),

time: 55.5 us -> 52.9 us (0.953)
  Pallas kernels: 54.8 us -> 52.2 us
    pallas_call x1, Pallas kernels: 53.9 us -> 51.3 us  [local(): pl.pallas_call(functools.partial(kernel, dims), out_shape=(jax.ShapeDtype...]
where the time goes in v3:
time: 52.9 us; the launch traced here: 52.8 us
  Pallas kernels  52.2 us (99%)
  between operations  0.64 us (1%)
    pallas_call x1, Pallas kernels, local(): pl.pallas_call(functools.partial(kernel, dims), out_shape=(jax.ShapeDtype...  51.3 us

profile of v3, /device:TPU:1, one launch (start us, length us, event | category | flops | bytes accessed | tf_op | source)
XLA Modules:
  0.0 52.8 jit_solution(10504062237095799334)
XLA Ops:
  0.6 51.3 %hull_leapfrog.1 = (f32[16,64,128]{2,1,0:T(8,128)S(1)}, f32[512,128]{1,0:T(8,128)S(1)}) custom-call(f32[16,64,128]{2,1,0:T(8,128)} %p_hbm.1, f32[16,64,128]{2,1,0:T(8,128)} %prev_hbm.1, f32[16,64,128]{2,1,0:T(8,128)} %b_hbm.1, f32[16,64,128]{2,1,0:T(8,128)} %kap_hbm.1, f32[512,128]{1,0:T(8,128)} %hull_hbm.1, s32[1,512]{1,0:T(1,128)} %bitcast.2, s32[1,512]{1,0:T(1,128)} %bitcast.3), custom_call_target="tpu_custom_call" | custom-call | tf_op jit(solution)/shard_map/hull_leapfrog/pallas_call | solution.py:586
  51.9 0.9 %write_out.1 = (f32[16,64,128]{2,1,0:T(8,128)}, f32[512,128]{1,0:T(8,128)}) custom-call(f32[16,64,128]{2,1,0:T(8,128)S(1)} %get-tuple-element.4.field, f32[512,128]{1,0:T(8,128)S(1)} %get-tuple-element.5.rows), custom_call_target="tpu_custom_call" | custom-call | tf_op jit(solution)/shard_map/write_out/pallas_call | solution.py:638

commit v4 on v3

--- a/solution.py
+++ b/solution.py
@@ -62,8 +62,8 @@
     p_hbm, prev_hbm, b_hbm, kap_hbm, hull_hbm, rb_hbm, rc_hbm,
     out_ref, hp_ref,
     E, EB, E2, ZS, ZR, SPLIT, ZW, ZB, PREV, KAP, HULL, FX, FY, TOT, BX, BY, BZ, NEXT,
-    CS, CR, CA, MC, SB, RV, ROWS, PK, RET, Q, QT, PM, RB, RC,
-    in_sem, hs_sem, hr_sem, cs_sem, cr_sem, fs_sem, fr_sem, as_sem, ar_sem, bs_sem, br_sem, self_sem,
+    CS, CR, CA, MC, SB, RV, ROWS, PK, RET, Q, QT, PM, RB, RC, RLP, RLB,
+    in_sem, hs_sem, hr_sem, ls_sem, lr_sem, lf_sem, cs_sem, cr_sem, fs_sem, fr_sem, as_sem, ar_sem, bs_sem, br_sem, self_sem,
 ):
     nz, nx, ny = dims
     NB = nz * nx * ny
@@ -201,14 +201,70 @@
 
     pl.semaphore_wait(barrier, NB)
 
+    QY = Y // nx
+    up_seam = (xi == nx - 1) & (zi < nz - 1)
+    down_seam = (xi == 0) & (zi > 0)
+    relay_up = (xi > 0) & (zi > 0)
+    relay_down = (xi < nx - 1) & (zi < nz - 1)
+    z_above, z_below = jnp.minimum(zi + 1, nz - 1), jnp.maximum(zi - 1, 0)
+
+    def seams(ref, field, width, relay):
+        lo = width
+        copies = []
+        for c in range(nx):
+            band_y = pl.ds(8 + c * QY, QY)
+            ends_here = c == 0
+            copies.append((up_seam, pltpu.make_async_remote_copy(
+                ref.at[pl.ds(X + lo - width, width), band_y],
+                ref.at[pl.ds(lo - width, width), band_y] if ends_here else relay.at[0],
+                ls_sem.at[field, 0, c], hr_sem.at[field, 0] if ends_here else lr_sem.at[field, 0],
+                device_id=(z_above * nx + c, gy, blk), device_id_type=MESH)))
+            ends_here = c == nx - 1
+            copies.append((down_seam, pltpu.make_async_remote_copy(
+                ref.at[pl.ds(lo, width), band_y],
+                ref.at[pl.ds(X + lo, width), band_y] if ends_here else relay.at[1],
+                ls_sem.at[field, 1, c], hr_sem.at[field, 1] if ends_here else lr_sem.at[field, 1],
+                device_id=(z_below * nx + c, gy, blk), device_id_type=MESH)))
+        band_x = pl.ds(8 + xi * QY, QY)
+        onward = [
+            (relay_up, 0, pltpu.make_async_remote_copy(
+                relay.at[0], ref.at[pl.ds(lo - width, width), band_x],
+                lf_sem.at[field, 0], hr_sem.at[field, 0],
+                device_id=(zi * nx, gy, blk), device_id_type=MESH)),
+            (relay_down, 1, pltpu.make_async_remote_copy(
+                relay.at[1], ref.at[pl.ds(X + lo, width), band_x],
+                lf_sem.at[field, 1], hr_sem.at[field, 1],
+                device_id=(zi * nx + nx - 1, gy, blk), device_id_type=MESH)),
+        ]
+
+        def begin():
+            for on, copy in copies:
+                pl.when(on)(lambda copy=copy: copy.start())
+
+        def forward():
+            for on, way, copy in onward:
+                @pl.when(on)
+                def _(way=way, copy=copy):
+                    drained(relay.at[way], lr_sem.at[field, way])
+                    copy.start()
+
+        def end():
+            for on, copy in copies:
+                pl.when(on)(lambda copy=copy: copy.wait_send())
+            for on, _, copy in onward:
+                pl.when(on)(lambda copy=copy: copy.wait_send())
+
+        return begin, forward, end
+
     def shares(ref, field, width):
         lo = width
         send, recv = hs_sem.at[field], hr_sem.at[field]
+        whole = field == 2
         return [
-            (gx < n_gx - 1, gx > 0, pltpu.make_async_remote_copy(
+            (gx < n_gx - 1 if whole else xi < nx - 1, gx > 0, pltpu.make_async_remote_copy(
                 ref.at[pl.ds(X + lo - width, width), pl.ds(8, Y)], ref.at[pl.ds(lo - width, width), pl.ds(8, Y)],
                 send.at[0], recv.at[0], device_id=(jnp.minimum(gx + 1, n_gx - 1), gy, blk), device_id_type=MESH)),
-            (gx > 0, gx < n_gx - 1, pltpu.make_async_remote_copy(
+            (gx > 0 if whole else xi > 0, gx < n_gx - 1, pltpu.make_async_remote_copy(
                 ref.at[pl.ds(lo, width), pl.ds(8, Y)], ref.at[pl.ds(X + lo, width), pl.ds(8, Y)],
                 send.at[1], recv.at[1], device_id=(jnp.maximum(gx - 1, 0), gy, blk), device_id_type=MESH)),
             (gy < ny - 1, gy > 0, pltpu.make_async_remote_copy(
@@ -251,6 +307,10 @@
 
     halo_p = shares(E, 0, 3)
     halo_b = shares(EB, 1, 2)
+    seam_p = seams(E, 0, 3, RLP)
+    seam_b = seams(EB, 1, 2, RLB)
+    seam_p[0]()
+    seam_b[0]()
     start(halo_p)
     start(halo_b)
 
@@ -272,6 +332,8 @@
         ).start()
     own_tile = pltpu.make_async_copy(CR, CA.at[0], self_sem.at[2])
     own_tile.start()
+    seam_p[1]()
+    seam_b[1]()
 
     rel_z = (placing // GS + (nz - zi)) % nz
     rel_x = (placing // (CAP * ny) % nx + (nx - xi)) % nx
@@ -422,6 +484,9 @@
         return 0
 
     lax.fori_loop(0, X // PER, first, 0)
+
+    seam_p[2]()
+    seam_b[2]()
 
     drained(CA.at[pl.ds(0, G - 1)], fr_sem)
     own_tile.wait()
@@ -624,7 +689,9 @@
                 V((HR, NB * CAP), BF16),
                 V((1, HR), jnp.int32),
                 V((1, HR), jnp.int32),
-                dma((7,)), dma((3, 5)), dma((3, 5)),
+                V((2, 3, Y // dims[1], Z), F32),
+                V((2, 2, Y // dims[1], Z), F32),
+                dma((7,)), dma((3, 5)), dma((3, 5)), dma((2, 2, dims[1])), dma((2, 2)), dma((2, 2)),
                 dma, dma, dma, dma, dma, dma((4,)), dma, dma((4,)), dma((4,)),
             ],
             compiler_params=pltpu.CompilerParams(collective_id=0, has_side_effects=True, vmem_limit_bytes=36 * 1024 * 1024),

time: 52.9 us -> 52.3 us (0.989)
  Pallas kernels: 52.2 us -> 51.5 us
    pallas_call x1, Pallas kernels: 51.3 us -> 50.6 us  [local(): pl.pallas_call(functools.partial(kernel, dims), out_shape=(jax.ShapeDtype...]
where the time goes in v4:
time: 52.3 us; the launch traced here: 52.2 us
  Pallas kernels  51.5 us (98%)
  between operations  0.64 us (1%)
    pallas_call x1, Pallas kernels, local(): pl.pallas_call(functools.partial(kernel, dims), out_shape=(jax.ShapeDtype...  50.6 us

profile of v4, /device:TPU:1, one launch (start us, length us, event | category | flops | bytes accessed | tf_op | source)
XLA Modules:
  0.0 52.2 jit_solution(12684973358308304666)
XLA Ops:
  0.6 50.6 %hull_leapfrog.1 = (f32[16,64,128]{2,1,0:T(8,128)S(1)}, f32[512,128]{1,0:T(8,128)S(1)}) custom-call(f32[16,64,128]{2,1,0:T(8,128)} %p_hbm.1, f32[16,64,128]{2,1,0:T(8,128)} %prev_hbm.1, f32[16,64,128]{2,1,0:T(8,128)} %b_hbm.1, f32[16,64,128]{2,1,0:T(8,128)} %kap_hbm.1, f32[512,128]{1,0:T(8,128)} %hull_hbm.1, s32[1,512]{1,0:T(1,128)} %bitcast.2, s32[1,512]{1,0:T(1,128)} %bitcast.3), custom_call_target="tpu_custom_call" | custom-call | tf_op jit(solution)/shard_map/hull_leapfrog/pallas_call | solution.py:651
  51.3 0.9 %write_out.1 = (f32[16,64,128]{2,1,0:T(8,128)}, f32[512,128]{1,0:T(8,128)}) custom-call(f32[16,64,128]{2,1,0:T(8,128)S(1)} %get-tuple-element.4.field, f32[512,128]{1,0:T(8,128)S(1)} %get-tuple-element.5.rows), custom_call_target="tpu_custom_call" | custom-call | tf_op jit(solution)/shard_map/write_out/pallas_call | solution.py:705

commit v5 on v4

--- a/solution.py
+++ b/solution.py
@@ -198,6 +198,29 @@
     gather_edge(1)
     all_planes(E, 3)
     gather_edge(0)
+
+    rel_z = (placing // GS + (nz - zi)) % nz
+    rel_x = (placing // (CAP * ny) % nx + (nx - xi)) % nx
+    rel_y = (placing // CAP % ny + (ny - gy)) % ny
+    relative = ((rel_z * nx + rel_x) * ny + rel_y) * CAP + placing % CAP
+    weights_row = lax.broadcasted_iota(jnp.int32, (16, LANES), 0)
+    place_row = lax.broadcasted_iota(jnp.int32, (16, HR), 0)
+    place_code = jnp.where(
+        place_row == 0, jnp.broadcast_to(relative // 32, (16, HR)),
+        jnp.where(place_row == 1, jnp.broadcast_to(relative % 32, (16, HR)), 0),
+    ).astype(F32).astype(BF16)
+    place_w = jnp.where(weights_row == 0, 32.0, jnp.where(weights_row == 1, 1.0, 0.0)).astype(BF16)
+    placing_col = dot_tn(place_code, place_w)
+    span = min(LANES, NB * CAP)
+    for m in range(NB * CAP // span):
+        spot_lane = lax.broadcasted_iota(jnp.int32, (8, span), 1)
+        label = spot_lane % CAP
+        for j in range(span // CAP):
+            dz, dx, dy = slots[m * (span // CAP) + j]
+            base = ((dz * nx + dx) * ny + dy) * CAP
+            label = jnp.where(spot_lane // CAP == j, label + base, label)
+        label = jnp.broadcast_to(label[0:1], (HR, span)).astype(F32)
+        PM[:, m * span : (m + 1) * span] = onehot(placing_col[:, :span] == label)
 
     pl.semaphore_wait(barrier, NB)
 
@@ -323,41 +346,6 @@
     own = pltpu.make_async_copy(SB.at[me], RV.at[NB - 1], self_sem.at[1])
     own.start()
 
-    drained(CR.at[pl.ds(0, nz - 1)], cr_sem)
-    own_col.wait()
-    for dx, dy in plane[1:]:
-        pltpu.make_async_remote_copy(
-            CR, CA.at[dx * ny + dy], fs_sem, fr_sem,
-            device_id=(zi * nx + xs[dx], ys[dy], blk), device_id_type=MESH,
-        ).start()
-    own_tile = pltpu.make_async_copy(CR, CA.at[0], self_sem.at[2])
-    own_tile.start()
-    seam_p[1]()
-    seam_b[1]()
-
-    rel_z = (placing // GS + (nz - zi)) % nz
-    rel_x = (placing // (CAP * ny) % nx + (nx - xi)) % nx
-    rel_y = (placing // CAP % ny + (ny - gy)) % ny
-    relative = ((rel_z * nx + rel_x) * ny + rel_y) * CAP + placing % CAP
-    weights_row = lax.broadcasted_iota(jnp.int32, (16, LANES), 0)
-    place_row = lax.broadcasted_iota(jnp.int32, (16, HR), 0)
-    place_code = jnp.where(
-        place_row == 0, jnp.broadcast_to(relative // 32, (16, HR)),
-        jnp.where(place_row == 1, jnp.broadcast_to(relative % 32, (16, HR)), 0),
-    ).astype(F32).astype(BF16)
-    place_w = jnp.where(weights_row == 0, 32.0, jnp.where(weights_row == 1, 1.0, 0.0)).astype(BF16)
-    placing_col = dot_tn(place_code, place_w)
-    span = min(LANES, NB * CAP)
-    for m in range(NB * CAP // span):
-        spot_lane = lax.broadcasted_iota(jnp.int32, (8, span), 1)
-        label = spot_lane % CAP
-        for j in range(span // CAP):
-            dz, dx, dy = slots[m * (span // CAP) + j]
-            base = ((dz * nx + dx) * ny + dy) * CAP
-            label = jnp.where(spot_lane // CAP == j, label + base, label)
-        label = jnp.broadcast_to(label[0:1], (HR, span)).astype(F32)
-        PM[:, m * span : (m + 1) * span] = onehot(placing_col[:, :span] == label)
-
     w_row = lax.broadcasted_iota(jnp.int32, (2 * LANES, LANES), 0) % LANES
     w_col = lax.broadcasted_iota(jnp.int32, (2 * LANES, LANES), 1)
 
@@ -417,9 +405,53 @@
         for i in range(PER):
             TOT[q * PER + i] = TOT[q * PER + i] + val[i]
 
+    inner_lane = lax.broadcasted_iota(jnp.int32, (Y, LANES), 1) < LANES - 1
+
+    def face_x(c):
+        BX[c] = (EB[c, 8 : 8 + Y] + EB[c + 1, 8 : 8 + Y]) * FACE
+
+    def own_faces(q, _):
+        for i in range(PER):
+            c = q * PER + i
+            own_b = EB[c + 2, 8 : 8 + Y]
+            BZ[c] = jnp.where(inner_lane, own_b + pltpu.roll(own_b, LANES - 1, 1), 0.0) * FACE
+        return 0
+
+    def flux_x(src, c):
+        FX[c] = wide(src[c, 8 : 8 + Y], src[c + 1, 8 : 8 + Y], src[c + 2, 8 : 8 + Y], src[c + 3, 8 : 8 + Y]) * BX[c]
+
+    def inner_x(src):
+        for c in range(3, X):
+            flux_x(src, c)
+
+    def outer_x(src):
+        for c in (0, 1, 2, X, X + 1, X + 2):
+            flux_x(src, c)
+
+    def across_y(src, c, i):
+        FY[i] = wide(src[c + 3, 5 : 13 + Y], src[c + 3, 6 : 14 + Y], src[c + 3, 7 : 15 + Y], src[c + 3, 8 : 16 + Y]) * BY[c]
+        return wide(FY[i, 0:Y], FY[i, 1 : 1 + Y], FY[i, 2 : 2 + Y], FY[i, 3 : 3 + Y])
+
+    lax.fori_loop(0, X // PER, own_faces, 0)
+    for c in range(3, X):
+        face_x(c)
+    inner_x(E)
+    for q in range(X // PER):
+        along_z(q)
+
+    drained(CR.at[pl.ds(0, nz - 1)], cr_sem)
+    own_col.wait()
+    for dx, dy in plane[1:]:
+        pltpu.make_async_remote_copy(
+            CR, CA.at[dx * ny + dy], fs_sem, fr_sem,
+            device_id=(zi * nx + xs[dx], ys[dy], blk), device_id_type=MESH,
+        ).start()
+    own_tile = pltpu.make_async_copy(CR, CA.at[0], self_sem.at[2])
+    own_tile.start()
+    seam_p[1]()
+    seam_b[1]()
+
     finish(halo_b)
-
-    inner_lane = lax.broadcasted_iota(jnp.int32, (Y, LANES), 1) < LANES - 1
     b_left = [ZR[1, r : r + 1] * left_on for r in (1, 2)]
     b_right = [ZR[1, r : r + 1] * right_on for r in (0, 1)]
     own_edge = [ZS[1, r : r + 1] for r in range(3, 7)]
@@ -435,34 +467,16 @@
         ],
         axis=0,
     )
-
-    def faces(q, _):
+    for c in (0, 1, 2, X, X + 1, X + 2):
+        face_x(c)
+
+    def faces_y(q, _):
         for i in range(PER):
             c = q * PER + i
-            BX[c] = (EB[c, 8 : 8 + Y] + EB[c + 1, 8 : 8 + Y]) * FACE
             BY[c] = (EB[c + 2, 6 : 14 + Y] + EB[c + 2, 7 : 15 + Y]) * FACE
-            own_b = EB[c + 2, 8 : 8 + Y]
-            BZ[c] = jnp.where(inner_lane, own_b + pltpu.roll(own_b, LANES - 1, 1), 0.0) * FACE
         return 0
 
-    lax.fori_loop(0, X // PER, faces, 0)
-    for c in range(X, X + 3):
-        BX[c] = (EB[c, 8 : 8 + Y] + EB[c + 1, 8 : 8 + Y]) * FACE
-
-    def flux_x(src, c):
-        FX[c] = wide(src[c, 8 : 8 + Y], src[c + 1, 8 : 8 + Y], src[c + 2, 8 : 8 + Y], src[c + 3, 8 : 8 + Y]) * BX[c]
-
-    def inner_x(src):
-        for c in range(3, X):
-            flux_x(src, c)
-
-    def outer_x(src):
-        for c in (0, 1, 2, X, X + 1, X + 2):
-            flux_x(src, c)
-
-    def across_y(src, c, i):
-        FY[i] = wide(src[c + 3, 5 : 13 + Y], src[c + 3, 6 : 14 + Y], src[c + 3, 7 : 15 + Y], src[c + 3, 8 : 16 + Y]) * BY[c]
-        return wide(FY[i, 0:Y], FY[i, 1 : 1 + Y], FY[i, 2 : 2 + Y], FY[i, 3 : 3 + Y])
+    lax.fori_loop(0, X // PER, faces_y, 0)
 
     def laplace(c):
         return TOT[c] + wide(FX[c], FX[c + 1], FX[c + 2], FX[c + 3])
@@ -470,11 +484,9 @@
     loads[5].wait()
     loads[6].wait()
     finish(halo_p)
-    inner_x(E)
     outer_x(E)
     fixes = fix_z(0)
     for q in range(X // PER):
-        along_z(q)
         add_fix(fixes, q)
 
     def first(q, _):

time: 52.3 us -> 52.2 us (level)
  no operation moved by 1% of the time
where the time goes in v5:
time: 52.2 us
  Pallas kernels  51.5 us (99%)
  between operations  0.64 us (1%)
    pallas_call x1, Pallas kernels, local(): pl.pallas_call(functools.partial(kernel, dims), out_shape=(jax.ShapeDtype...  50.6 us

profile of v5, /device:TPU:1, one launch (start us, length us, event | category | flops | bytes accessed | tf_op | source)
XLA Modules:
  0.0 52.2 jit_solution(4111131450108974233)
XLA Ops:
  0.6 50.6 %hull_leapfrog.1 = (f32[16,64,128]{2,1,0:T(8,128)S(1)}, f32[512,128]{1,0:T(8,128)S(1)}) custom-call(f32[16,64,128]{2,1,0:T(8,128)} %p_hbm.1, f32[16,64,128]{2,1,0:T(8,128)} %prev_hbm.1, f32[16,64,128]{2,1,0:T(8,128)} %b_hbm.1, f32[16,64,128]{2,1,0:T(8,128)} %kap_hbm.1, f32[512,128]{1,0:T(8,128)} %hull_hbm.1, s32[1,512]{1,0:T(1,128)} %bitcast.2, s32[1,512]{1,0:T(1,128)} %bitcast.3), custom_call_target="tpu_custom_call" | custom-call | tf_op jit(solution)/shard_map/hull_leapfrog/pallas_call | solution.py:663
  51.3 0.9 %write_out.1 = (f32[16,64,128]{2,1,0:T(8,128)}, f32[512,128]{1,0:T(8,128)}) custom-call(f32[16,64,128]{2,1,0:T(8,128)S(1)} %get-tuple-element.4.field, f32[512,128]{1,0:T(8,128)S(1)} %get-tuple-element.5.rows), custom_call_target="tpu_custom_call" | custom-call | tf_op jit(solution)/shard_map/write_out/pallas_call | solution.py:717

commit v6 on v5

--- a/solution.py
+++ b/solution.py
@@ -332,19 +332,23 @@
     halo_b = shares(EB, 1, 2)
     seam_p = seams(E, 0, 3, RLP)
     seam_b = seams(EB, 1, 2, RLB)
+    start(halo_p[2:])
+    start(halo_b[2:])
+
+    def send_rows(some):
+        for k in some:
+            dz, dx, dy = slots[k]
+            dest_gx = zs[dz] * nx + xs[dx]
+            pltpu.make_async_remote_copy(
+                SB.at[dest_gx * ny + ys[dy]], RV.at[k], as_sem, ar_sem.at[group_of(k)],
+                device_id=(dest_gx, ys[dy], blk), device_id_type=MESH,
+            ).start()
+
+    send_rows(range(NB // 2))
     seam_p[0]()
     seam_b[0]()
-    start(halo_p)
-    start(halo_b)
-
-    for k, (dz, dx, dy) in enumerate(slots[:-1]):
-        dest_gx = zs[dz] * nx + xs[dx]
-        pltpu.make_async_remote_copy(
-            SB.at[dest_gx * ny + ys[dy]], RV.at[k], as_sem, ar_sem.at[group_of(k)],
-            device_id=(dest_gx, ys[dy], blk), device_id_type=MESH,
-        ).start()
-    own = pltpu.make_async_copy(SB.at[me], RV.at[NB - 1], self_sem.at[1])
-    own.start()
+    start(halo_p[0:2])
+    start(halo_b[0:2])
 
     w_row = lax.broadcasted_iota(jnp.int32, (2 * LANES, LANES), 0) % LANES
     w_col = lax.broadcasted_iota(jnp.int32, (2 * LANES, LANES), 1)
@@ -448,10 +452,11 @@
         ).start()
     own_tile = pltpu.make_async_copy(CR, CA.at[0], self_sem.at[2])
     own_tile.start()
-    seam_p[1]()
-    seam_b[1]()
-
-    finish(halo_b)
+    send_rows(range(NB // 2, NB - 1))
+    own = pltpu.make_async_copy(SB.at[me], RV.at[NB - 1], self_sem.at[1])
+    own.start()
+
+    finish(halo_b[2:])
     b_left = [ZR[1, r : r + 1] * left_on for r in (1, 2)]
     b_right = [ZR[1, r : r + 1] * right_on for r in (0, 1)]
     own_edge = [ZS[1, r : r + 1] for r in range(3, 7)]
@@ -467,9 +472,6 @@
         ],
         axis=0,
     )
-    for c in (0, 1, 2, X, X + 1, X + 2):
-        face_x(c)
-
     def faces_y(q, _):
         for i in range(PER):
             c = q * PER + i
@@ -481,24 +483,12 @@
     def laplace(c):
         return TOT[c] + wide(FX[c], FX[c + 1], FX[c + 2], FX[c + 3])
 
-    loads[5].wait()
-    loads[6].wait()
-    finish(halo_p)
-    outer_x(E)
+    finish(halo_p[2:])
     fixes = fix_z(0)
     for q in range(X // PER):
         add_fix(fixes, q)
-
-    def first(q, _):
-        for i in range(PER):
-            c = q * PER + i
-            E2[c + 3, 8 : 8 + Y] = 2.0 * E[c + 3, 8 : 8 + Y] - PREV[c] + KAP[c] * (laplace(c) + across_y(E, c, i))
-        return 0
-
-    lax.fori_loop(0, X // PER, first, 0)
-
-    seam_p[2]()
-    seam_b[2]()
+    seam_p[1]()
+    seam_b[1]()
 
     drained(CA.at[pl.ds(0, G - 1)], fr_sem)
     own_tile.wait()
@@ -529,6 +519,29 @@
 
     lax.fori_loop(0, nz, build_q, 0)
 
+    quads = X // PER
+    ends = sorted({0, quads - 1})
+    inside = [q for q in range(quads) if q not in ends]
+
+    def first(q):
+        for i in range(PER):
+            c = q * PER + i
+            E2[c + 3, 8 : 8 + Y] = 2.0 * E[c + 3, 8 : 8 + Y] - PREV[c] + KAP[c] * (laplace(c) + across_y(E, c, i))
+
+    loads[5].wait()
+    loads[6].wait()
+    for q in inside:
+        first(q)
+    finish(halo_b[0:2])
+    for c in (0, 1, 2, X, X + 1, X + 2):
+        face_x(c)
+    finish(halo_p[0:2])
+    outer_x(E)
+    for q in ends:
+        first(q)
+    seam_p[2]()
+    seam_b[2]()
+
     for n in range(parts_n):
         last = n == parts_n - 1
         drained(RV.at[pl.ds(0, share - 1 if last else share)], ar_sem.at[n])
@@ -549,9 +562,6 @@
             SPLIT[c * Y : (c + 1) * Y] = parts(mid)
             PREV[c] = force - E[c + 3, 8 : 8 + Y]
 
-    quads = X // PER
-    ends = sorted({0, quads - 1})
-    inside = [q for q in range(quads) if q not in ends]
     for q in ends:
         middle(q)
     start(halo_m[0:2])

time: 52.2 us -> 51.9 us (level)
  no operation moved by 1% of the time
where the time goes in v6:
time: 51.9 us; the launch traced here: 51.8 us
  Pallas kernels  51.2 us (99%)
  between operations  0.64 us (1%)
    pallas_call x1, Pallas kernels, local(): pl.pallas_call(functools.partial(kernel, dims), out_shape=(jax.ShapeDtype...  50.3 us

profile of v6, /device:TPU:1, one launch (start us, length us, event | category | flops | bytes accessed | tf_op | source)
XLA Modules:
  0.0 51.8 jit_solution(6655355334649512232)
XLA Ops:
  0.6 50.3 %hull_leapfrog.1 = (f32[16,64,128]{2,1,0:T(8,128)S(1)}, f32[512,128]{1,0:T(8,128)S(1)}) custom-call(f32[16,64,128]{2,1,0:T(8,128)} %p_hbm.1, f32[16,64,128]{2,1,0:T(8,128)} %prev_hbm.1, f32[16,64,128]{2,1,0:T(8,128)} %b_hbm.1, f32[16,64,128]{2,1,0:T(8,128)} %kap_hbm.1, f32[512,128]{1,0:T(8,128)} %hull_hbm.1, s32[1,512]{1,0:T(1,128)} %bitcast.2, s32[1,512]{1,0:T(1,128)} %bitcast.3), custom_call_target="tpu_custom_call" | custom-call | tf_op jit(solution)/shard_map/hull_leapfrog/pallas_call | solution.py:673
  50.9 0.9 %write_out.1 = (f32[16,64,128]{2,1,0:T(8,128)}, f32[512,128]{1,0:T(8,128)}) custom-call(f32[16,64,128]{2,1,0:T(8,128)S(1)} %get-tuple-element.4.field, f32[512,128]{1,0:T(8,128)S(1)} %get-tuple-element.5.rows), custom_call_target="tpu_custom_call" | custom-call | tf_op jit(solution)/shard_map/write_out/pallas_call | solution.py:727

commit v7 on v6

--- a/solution.py
+++ b/solution.py
@@ -344,11 +344,13 @@
                 device_id=(dest_gx, ys[dy], blk), device_id_type=MESH,
             ).start()
 
-    send_rows(range(NB // 2))
     seam_p[0]()
     seam_b[0]()
     start(halo_p[0:2])
     start(halo_b[0:2])
+    send_rows(range(NB - 1))
+    own = pltpu.make_async_copy(SB.at[me], RV.at[NB - 1], self_sem.at[1])
+    own.start()
 
     w_row = lax.broadcasted_iota(jnp.int32, (2 * LANES, LANES), 0) % LANES
     w_col = lax.broadcasted_iota(jnp.int32, (2 * LANES, LANES), 1)
@@ -452,9 +454,6 @@
         ).start()
     own_tile = pltpu.make_async_copy(CR, CA.at[0], self_sem.at[2])
     own_tile.start()
-    send_rows(range(NB // 2, NB - 1))
-    own = pltpu.make_async_copy(SB.at[me], RV.at[NB - 1], self_sem.at[1])
-    own.start()
 
     finish(halo_b[2:])
     b_left = [ZR[1, r : r + 1] * left_on for r in (1, 2)]

time: 51.9 us -> 52.3 us (level)
  no operation moved by 1% of the time
where the time goes in v7:
time: 52.3 us; the launch traced here: 52.2 us
  Pallas kernels  51.5 us (98%)
  between operations  0.64 us (1%)
    pallas_call x1, Pallas kernels, local(): pl.pallas_call(functools.partial(kernel, dims), out_shape=(jax.ShapeDtype...  50.6 us

profile of v7, /device:TPU:1, one launch (start us, length us, event | category | flops | bytes accessed | tf_op | source)
XLA Modules:
  0.0 52.2 jit_solution(16880601071955850236)
XLA Ops:
  0.6 50.6 %hull_leapfrog.1 = (f32[16,64,128]{2,1,0:T(8,128)S(1)}, f32[512,128]{1,0:T(8,128)S(1)}) custom-call(f32[16,64,128]{2,1,0:T(8,128)} %p_hbm.1, f32[16,64,128]{2,1,0:T(8,128)} %prev_hbm.1, f32[16,64,128]{2,1,0:T(8,128)} %b_hbm.1, f32[16,64,128]{2,1,0:T(8,128)} %kap_hbm.1, f32[512,128]{1,0:T(8,128)} %hull_hbm.1, s32[1,512]{1,0:T(1,128)} %bitcast.2, s32[1,512]{1,0:T(1,128)} %bitcast.3), custom_call_target="tpu_custom_call" | custom-call | tf_op jit(solution)/shard_map/hull_leapfrog/pallas_call | solution.py:672
  51.3 0.9 %write_out.1 = (f32[16,64,128]{2,1,0:T(8,128)}, f32[512,128]{1,0:T(8,128)}) custom-call(f32[16,64,128]{2,1,0:T(8,128)S(1)} %get-tuple-element.4.field, f32[512,128]{1,0:T(8,128)S(1)} %get-tuple-element.5.rows), custom_call_target="tpu_custom_call" | custom-call | tf_op jit(solution)/shard_map/write_out/pallas_call | solution.py:726

commit v8 on v6

--- a/solution.py
+++ b/solution.py
@@ -344,7 +344,7 @@
                 device_id=(dest_gx, ys[dy], blk), device_id_type=MESH,
             ).start()
 
-    send_rows(range(NB // 2))
+    send_rows(range(NB // 8))
     seam_p[0]()
     seam_b[0]()
     start(halo_p[0:2])
@@ -452,7 +452,7 @@
         ).start()
     own_tile = pltpu.make_async_copy(CR, CA.at[0], self_sem.at[2])
     own_tile.start()
-    send_rows(range(NB // 2, NB - 1))
+    send_rows(range(NB // 8, NB - 1))
     own = pltpu.make_async_copy(SB.at[me], RV.at[NB - 1], self_sem.at[1])
     own.start()
 

time: 51.9 us -> 52.2 us (level)
  no operation moved by 1% of the time
where the time goes in v8:
time: 52.2 us; the launch traced here: 52.1 us
  Pallas kernels  51.5 us (99%)
  between operations  0.64 us (1%)
    pallas_call x1, Pallas kernels, local(): pl.pallas_call(functools.partial(kernel, dims), out_shape=(jax.ShapeDtype...  50.6 us

profile of v8, /device:TPU:1, one launch (start us, length us, event | category | flops | bytes accessed | tf_op | source)
XLA Modules:
  0.0 52.1 jit_solution(11815789696008904349)
XLA Ops:
  0.6 50.6 %hull_leapfrog.1 = (f32[16,64,128]{2,1,0:T(8,128)S(1)}, f32[512,128]{1,0:T(8,128)S(1)}) custom-call(f32[16,64,128]{2,1,0:T(8,128)} %p_hbm.1, f32[16,64,128]{2,1,0:T(8,128)} %prev_hbm.1, f32[16,64,128]{2,1,0:T(8,128)} %b_hbm.1, f32[16,64,128]{2,1,0:T(8,128)} %kap_hbm.1, f32[512,128]{1,0:T(8,128)} %hull_hbm.1, s32[1,512]{1,0:T(1,128)} %bitcast.2, s32[1,512]{1,0:T(1,128)} %bitcast.3), custom_call_target="tpu_custom_call" | custom-call | tf_op jit(solution)/shard_map/hull_leapfrog/pallas_call | solution.py:673
  51.2 0.9 %write_out.1 = (f32[16,64,128]{2,1,0:T(8,128)}, f32[512,128]{1,0:T(8,128)}) custom-call(f32[16,64,128]{2,1,0:T(8,128)S(1)} %get-tuple-element.4.field, f32[512,128]{1,0:T(8,128)S(1)} %get-tuple-element.5.rows), custom_call_target="tpu_custom_call" | custom-call | tf_op jit(solution)/shard_map/write_out/pallas_call | solution.py:727
